TPU v7x, 256 devices: a whole 4x4x8 slice. The times are simulated.
256 devices in a mesh: row: 8 (over y, core), col: 32 (over z, x).
Axes of the slice: x: 4, y: 4, z: 8, core: 2. Of those that a mesh axis runs over, the one named last changes fastest.
Arguments:
- hidden: bfloat16 [1024, 24576], P(None, 'row'), may hold values from -6 to 6
- down_weight: bfloat16 [24576, 6144], P('row', 'col'), may hold values from -0.0390625 to 0.0390625
- residual: bfloat16 [1024, 6144], P('row', 'col'), may hold values from -260 to 260
- gain: bfloat16 [6144], P('col'), may hold values from 0.099609375 to 1.8984375
- qk_weight: bfloat16 [6144, 12288], P(None, 'col'), may hold values from -0.078125 to 0.078125
Outputs:
- stream: bfloat16 [1024, 6144], P('row', 'col')
- queries_keys: bfloat16 [1024, 12288], P('row', 'col')
All inputs are finite; a program needn't handle non-finite values.
Results may differ from a plain program's by a relative error of at most 0.015.
Values may be sent and summed in bfloat16 or wider, within the bound.
A program may use at most 64 MiB of HBM per device.

v0:
```python
import jax
import jax.numpy as jnp
from jax import lax
from jax.sharding import PartitionSpec as P


def joined(value, axis, join):
    pieces = jax.tree.map(lambda part: lax.all_gather(part, axis), value)
    head = jax.tree.map(lambda part: part[0], pieces)
    tail = jax.tree.map(lambda part: part[1:], pieces)
    total, _ = lax.scan(lambda total, section: (join(total, section), None), head, tail)
    return total


def combine_moments(first, second):
    count_a, mean_a, spread_a = first
    count_b, mean_b, spread_b = second
    count = count_a + count_b
    delta = mean_b - mean_a
    mean = mean_a + delta * count_b / count
    spread = spread_a + spread_b + delta * delta * count_a * count_b / count
    return (count, mean, spread)


def per_device(hidden, down_weight, residual, gain, qk_weight):
    tok_rows = residual.shape[0]
    mlp = lax.psum_scatter(
        jnp.dot(hidden, down_weight, preferred_element_type=jnp.float32).astype(jnp.bfloat16),
        "row",
        scatter_dimension=0,
        tiled=True,
    ).astype(jnp.float32)
    stream = (residual.astype(jnp.float32) + mlp).astype(jnp.bfloat16)
    values = stream.astype(jnp.float32)
    local_width = values.shape[1]
    local_mean = jnp.mean(values, axis=1)
    local_dev = values - local_mean[:, None]
    local_spread = jnp.sum(local_dev * local_dev, axis=1)
    counts = jnp.full((tok_rows,), float(local_width), jnp.float32)
    total_count, mean_flat, spread_flat = joined(
        (counts, local_mean, local_spread), "col", combine_moments
    )
    mean = mean_flat[:, None]
    var = (spread_flat / total_count)[:, None]
    normed = ((values - mean) / jnp.sqrt(var + 1e-06) * gain.astype(jnp.float32)[None, :]).astype(
        jnp.bfloat16
    )
    product = jnp.dot(
        lax.all_gather(normed, "col", axis=1, tiled=True),
        qk_weight,
        preferred_element_type=jnp.float32,
    )
    return (stream, product.astype(jnp.bfloat16))


def solution(mesh):
    placed = (P(None, "row"), P("row", "col"), P("row", "col"), P("col"), P(None, "col"))
    return jax.shard_map(
        per_device,
        mesh=mesh,
        in_specs=placed,
        out_specs=(P("row", "col"), P("row", "col")),
        check_vma=False,
    )
```

profile of v0, /device:TPU:2, one launch (start us, length us, event | category | flops | bytes accessed | tf_op | source)
XLA Modules:
  0.0 213.7 jit_solution(6401340985521224175)
XLA Ops:
  7.2 0.0 copy-start
  7.2 0.0 copy-start.3
  7.2 0.0 copy-start.2
  7.2 0.0 reduce-scatter.4.cloned.1.call-start
  7.2 1.2 copy-done
  8.4 5.0 %convolution_convert_fusion = bf16[1024,192]{0,1:T(8,128)(2,1)S(1)} fusion(bf16[1024,3072]{1,0:T(8,128)(2,1)} %param.7, bf16[3072,192]{0,1:T(8,128)(2,1)S(1)} %copy-done), kind=kOutput, calls=%fused_computation.6 | convolution fusion | flops 1208156160 | bytes 7864320 | tf_op jit(solution)/shard_map/dot_general | solution.py:28
  13.4 1.0 copy.7
  14.4 0.0 reduce-scatter.4.cloned.1.call-update
  14.5 0.0 all-gather.6.cloned.1.call-start
  14.5 0.0 copy-done.3
  14.5 36.5 %reduce-scatter.4.cloned.1.call-done = bf16[128,192]{1,0:T(8,128)(2,1)} async-done(((bf16[1024,192]{1,0:T(8,128)(2,1)}), bf16[128,192]{1,0:T(8,128)(2,1)}) %reduce-scatter.4.cloned.1.call-update) | async-done | bytes 49168
  51.1 0.9 copy.8
  52.0 0.0 copy-done.2
  52.1 0.0 copy-start.1
  52.1 39.9 %all-gather.3 = f32[32,1,128]{2,1,0:T(1,128)S(1)} all-gather(f32[1,1,128]{2,1,0:T(1,128)S(1)} %bitcast.36), channel_id=3, replica_groups=mesh['row'=8,'col'=32] {'col'}, dimensions={0}, use_global_device_ids=true | all-gather | bytes 16896 | tf_op jit(solution)/shard_map/all_gather | solution.py:8
  92.1 36.5 %all-gather.2 = f32[32,1,128]{2,1,0:T(1,128)S(1)} all-gather(f32[1,1,128]{2,1,0:T(1,128)S(1)} %get-tuple-element.100), channel_id=2, replica_groups=mesh['row'=8,'col'=32] {'col'}, dimensions={0}, use_global_device_ids=true | all-gather | bytes 16896 | tf_op jit(solution)/shard_map/all_gather | solution.py:8
  128.6 2.0 while.16
  130.6 0.7 fusion.5
  131.3 0.0 all-gather.6.cloned.1.call-update
  131.3 71.1 %all-gather.6.cloned.1.call-done = bf16[128,6144]{0,1:T(8,128)(2,1)} async-done(((bf16[128,192]{0,1:T(8,128)(2,1)}), bf16[128,6144]{0,1:T(8,128)(2,1)}) %all-gather.6.cloned.1.call-update) | async-done | bytes 1572880 | tf_op jit(solution)/shard_map/all_gather | solution.py:49
  202.4 4.5 %convolution_convert_fusion.1 = bf16[128,384]{1,0:T(8,128)(2,1)} fusion(bf16[128,6144]{0,1:T(8,128)(2,1)} %all-gather.6.cloned.1.call-done, bf16[6144,384]{1,0:T(8,128)(2,1)} %param.11), kind=kOutput, calls=%fused_computation.7 | convolution fusion | flops 604028928 | bytes 6389760 | tf_op jit(solution)/shard_map/dot_general | solution.py:48
  206.9 0.0 copy-done.1
  (74 shorter events, 1.5 us)
Async XLA Ops:
  7.2 1.3 copy-start
  7.2 7.3 %copy-start.3 = (bf16[192]{0:T(256)(128)(2,1)S(1)}, bf16[192]{0:T(256)(128)(2,1)}, u32[]{:S(2)}) copy-start(bf16[192]{0:T(256)(128)(2,1)} %param.10) | copy-start | bytes 1156
  7.2 44.8 %copy-start.2 = (bf16[128,192]{0,1:T(8,128)(2,1)S(1)}, bf16[128,192]{0,1:T(8,128)(2,1)}, u32[]{:S(2)}) copy-start(bf16[128,192]{0,1:T(8,128)(2,1)} %param.9) | copy-start | bytes 147460
  7.2 43.9 %reduce-scatter.4.cloned.1.call-start = ((), (), s32[]{:S(2)}) async-start(), calls=%async_computation.2 | async-start | bytes 589824
  14.5 187.9 %all-gather.6.cloned.1.call-start = ((), (), s32[]{:S(2)}) async-start(), calls=%async_computation.1 | async-start | bytes 1622016 | tf_op jit(solution)/shard_map/all_gather | solution.py:49
  52.1 154.8 %copy-start.1 = (bf16[128,192]{0,1:T(8,128)(2,1)}, bf16[128,192]{0,1:T(8,128)(2,1)S(1)}, u32[]{:S(2)}) copy-start(bf16[128,192]{0,1:T(8,128)(2,1)S(1)} %get-tuple-element.98) | copy-start | bytes 147460
Sparse Core Ops, SparseCore 0:
  14.6 36.4 reduce-scatter.3
  131.4 70.9 all-gather.5
where the time goes:
time: 215 us; the launch traced here: 214 us
  waiting for transfers between devices  108 us (50%)
  blocking collectives  76.4 us (36%)
  between operations  14.1 us (7%)
  matrix products  9.47 us (4%)
  local copies, waits for them, and re-layouts  3.17 us (1%)
  other arithmetic  2.24 us (1%)
    all_gather x2, blocking collectives, joined(): pieces = jax.tree.map(lambda part: lax.all_gather(part, axis), value)  76.4 us
    all_gather x1, waiting for transfers between devices, per_device(): lax.all_gather(normed, 'col', axis=1, tiled=True)  71.1 us
    unnamed x3, waiting for transfers between devices  36.6 us
    dot_general x1, matrix products, per_device(): jnp.dot(hidden, down_weight, preferred_element_type=jnp.float32)  4.99 us
    dot_general x1, matrix products, per_device(): jnp.dot(lax.all_gather(normed, 'col', axis=1, tiled=True), qk_weight, pre...  4.48 us
  transfers between devices with their start and end apart: 2, of which 2 were waited for; matrix products, arithmetic and copies ran while one was open for 0% of the time, Pallas kernels for 0%

commit v1 on v0

v1 whole, which is shorter than its diff:
```python
import functools

import jax
import jax.numpy as jnp
from jax import lax
from jax.experimental import pallas as pl
from jax.experimental.pallas import tpu as pltpu
from jax.sharding import PartitionSpec as P

MESH = pl.DeviceIdType.MESH
F32, BF16 = jnp.float32, jnp.bfloat16
NX, NZ, NY = 4, 8, 4
ROWS, COLS = 2 * NY, NZ * NX
TOK, WIDE = 128, 128
NARROW = 64


def lanes(shape):
    return lax.broadcasted_iota(jnp.int32, shape, len(shape) - 1)


def kernel(
    hidden, down, residual, gain, weight, stream_out, qk_out,
    hid_v, down_a, down_n, down_b, res_v, gain_in, gains, w_v, stream_v, qk_v,
    rs_send, rs_recv, ga, gb,
    load_sem, rs_ssem, rs_rsem, gx_ssem, gx_rsem, gz_ssem, gz_rsem,
    a_rsem, a4_rsem, bx_rsem, bz_rsem, bz4_rsem, ag_ssem, out_sem,
):
    row, col = lax.axis_index("row"), lax.axis_index("col")
    y, core = row // 2, row % 2
    z, x = col // NX, col % NX

    def at(zz, xx):
        return (row, zz * NX + xx)

    def zs(d):
        return lax.rem(z + d + NZ, NZ)

    def xs(d):
        return lax.rem(x + d + NX, NX)

    def load(src, dst, sem):
        copy = pltpu.make_async_copy(src, dst, load_sem.at[sem])
        copy.start()
        return copy

    c_down_a = load(down.at[:, pl.ds(0, WIDE)], down_a, 0)
    c_down_n = load(down.at[:, pl.ds(WIDE, NARROW)], down_n, 1)
    c_hid = []
    order = (2, 1, 3, 0)
    for i, d in enumerate(order):
        rows = pl.ds(pl.multiple_of(lax.rem(y + d, NY) * 2 * TOK, 2 * TOK), 2 * TOK)
        c_hid.append(load(hidden.at[rows], hid_v.at[i], 2 + i))
    c_gain = load(gain, gain_in, 6)
    c_res = load(residual, res_v, 7)
    c_w = load(weight, w_v, 8)

    barrier = pltpu.get_barrier_semaphore()
    peers = [(lax.rem(row + d, ROWS), col) for d in range(1, ROWS)]
    peers += [at(z, xs(d)) for d in range(1, NX)]
    peers += [at(zs(d), x) for d in range(1, NZ)]
    for peer in peers:
        pl.semaphore_signal(barrier, inc=1, device_id=peer, device_id_type=MESH)

    c_gain.wait()
    g = gain_in[...].astype(F32)
    gn = g[:, WIDE:]
    gains[col] = jnp.concatenate([g[:, :WIDE], gn, gn], axis=1)
    pl.semaphore_wait(barrier, len(peers))

    def send(src, dst, ssem, rsem, peer):
        copy = pltpu.make_async_remote_copy(
            src_ref=src, dst_ref=dst, send_sem=ssem, recv_sem=rsem,
            device_id=peer, device_id_type=MESH,
        )
        copy.start()
        return copy

    def arrived(ref, rsem):
        pltpu.make_async_copy(ref, ref, rsem).wait()

    sends = []
    for d in range(1, NX):
        sends.append(send(gains.at[col], gains.at[col], gx_ssem.at[d - 1], gx_rsem.at[NX - 1 - d], at(z, xs(d))))

    c_down_n.wait()
    n = down_n[...]
    down_b[...] = jnp.concatenate([n, n], axis=1)
    c_down_a.wait()
    lane = lanes((NARROW, WIDE))
    own_a = own_b = None
    for i, d in enumerate(order):
        c_hid[i].wait()
        h = hid_v[i]
        pa = jnp.dot(h, down_a[...], preferred_element_type=F32)
        pb = jnp.dot(h, down_b[...], preferred_element_type=F32)
        yy = lax.rem(y + d, NY)
        for k in range(2):
            a = pa[k * TOK:(k + 1) * TOK]
            b = pb[k * TOK:(k + 1) * TOK]
            b = jnp.where(lane < NARROW, b[:NARROW], b[NARROW:])
            rs_send[2 * i + k, :TOK] = a.astype(BF16)
            rs_send[2 * i + k, TOK:] = b.astype(BF16)
        for k in range(2):
            peer = (yy * 2 + k, col)
            if d:
                sends.append(send(rs_send.at[2 * i + k], rs_recv.at[row], rs_ssem.at[2 * i + k], rs_rsem.at[row], peer))
            else:
                @pl.when(core != k)
                def _():
                    send(rs_send.at[2 * i + k], rs_recv.at[row], rs_ssem.at[2 * i + k], rs_rsem.at[row], peer)

                @pl.when(core == k)
                def _():
                    rs_recv[row] = rs_send[2 * i + k]

    for d in range(NX - 1):
        slot = z * NX + lax.rem(x + d + 1, NX)
        arrived(gains.at[slot], gx_rsem.at[d])
    four = gains.at[pl.ds(z * NX, NX)]
    for d in range(1, NZ):
        sends.append(send(four, four, gz_ssem.at[d - 1], gz_rsem.at[NZ - 1 - d], at(zs(d), x)))

    for d in range(1, ROWS):
        r = lax.rem(row + d, ROWS)
        arrived(rs_recv.at[r], rs_rsem.at[r])
    c_res.wait()
    res = res_v[...].astype(F32)
    total = jnp.zeros((TOK + NARROW, WIDE), F32)
    for r in range(ROWS):
        total = total + rs_recv[r].astype(F32)
    sa = (res[:, :WIDE] + total[:TOK]).astype(BF16)
    rb = jnp.concatenate([res[:NARROW, WIDE:], res[NARROW:, WIDE:]], axis=1)
    sb32 = rb + total[TOK:]
    sb = sb32.astype(BF16)
    ga[col] = sa
    gb[col] = sb

    nag = [0]

    def push(src, rsem, peer):
        sends.append(send(src, src, ag_ssem.at[nag[0]], rsem, peer))
        nag[0] += 1

    def slot_a(dz, dx):
        return zs(dz) * NX + xs(dx)

    half = pl.ds(0, TOK // 2), pl.ds(TOK // 2, TOK // 2)
    bhalf = pl.ds(0, NARROW // 2), pl.ds(NARROW // 2, NARROW // 2)

    push(gb.at[col], bx_rsem.at[0], at(z, xs(1)))
    push(gb.at[col], bx_rsem.at[1], at(z, xs(-1)))
    push(ga.at[col], a_rsem.at[col], at(zs(1), x))
    push(ga.at[col], a_rsem.at[col], at(zs(-1), x))
    push(ga.at[col], a_rsem.at[col], at(z, xs(1)))
    push(ga.at[col], a_rsem.at[col], at(z, xs(-1)))

    stream_v[:, :WIDE] = sa
    back = sb32.astype(BF16)
    stream_v[:NARROW, WIDE:] = back[:, :NARROW]
    stream_v[NARROW:, WIDE:] = back[:, NARROW:]
    c_stream = pltpu.make_async_copy(stream_v, stream_out, out_sem.at[0])
    c_stream.start()

    def a_from_z(d):
        if d < 4:
            for s in (-1, 1):
                slot = slot_a(s * d, 0)
                arrived(ga.at[slot], a_rsem.at[slot])
                if d < 3:
                    push(ga.at[slot], a_rsem.at[slot], at(zs(-s), x))
                else:
                    h = half[0] if s < 0 else half[1]
                    push(ga.at[slot, h], a4_rsem.at[0 if s < 0 else 1], at(zs(-s), x))
                push(ga.at[slot], a_rsem.at[slot], at(z, xs(1)))
                push(ga.at[slot], a_rsem.at[slot], at(z, xs(-1)))
        else:
            slot = slot_a(4, 0)
            for k in range(2):
                arrived(ga.at[slot, half[k]], a4_rsem.at[k])
            push(ga.at[slot], a_rsem.at[slot], at(z, xs(1)))
            push(ga.at[slot], a_rsem.at[slot], at(z, xs(-1)))

    def a_from_x(dz):
        for s in (-1, 1):
            slot = slot_a(dz, s)
            arrived(ga.at[slot], a_rsem.at[slot])
            h = half[0] if s < 0 else half[1]
            push(ga.at[slot, h], ax2_rsem(dz, 0 if s < 0 else 1), at(z, xs(-s)))

    def ax2_rsem(dz, k):
        return ax2.at[zs(dz), k]

    ax2 = bz4_rsem.at[pl.ds(1, NZ)]

    def a_relayed(dz):
        slot = slot_a(dz, 2)
        for k in range(2):
            arrived(ga.at[slot, half[k]], ax2_rsem(dz, k))

    def b_of(dz):
        return gb.at[pl.ds(zs(dz) * NX, NX)]

    def b_from_z(d):
        if d < 4:
            for s in (-1, 1):
                arrived(b_of(s * d), bz_rsem.at[zs(s * d)])
                if d < 3:
                    push(b_of(s * d), bz_rsem.at[zs(s * d)], at(zs(-s), x))
                else:
                    k = 0 if s < 0 else 1
                    part = gb.at[pl.ds(zs(s * d) * NX + 2 * k, 2)]
                    push(part, bz4_rsem.at[0, k], at(zs(-s), x))
        else:
            for k in range(2):
                part = gb.at[pl.ds(zs(4) * NX + 2 * k, 2)]
                arrived(part, bz4_rsem.at[0, k])

    left, right = z * NX + xs(-1), z * NX + xs(1)
    arrived(gb.at[left], bx_rsem.at[0])
    push(gb.at[left, bhalf[0]], bx_rsem.at[2], at(z, xs(1)))
    arrived(gb.at[right], bx_rsem.at[1])
    push(gb.at[right, bhalf[1]], bx_rsem.at[3], at(z, xs(-1)))
    a_from_z(1)
    a_from_x(0)
    far = z * NX + xs(2)
    arrived(gb.at[far, bhalf[0]], bx_rsem.at[2])
    arrived(gb.at[far, bhalf[1]], bx_rsem.at[3])
    push(b_of(0), bz_rsem.at[z], at(zs(1), x))
    push(b_of(0), bz_rsem.at[z], at(zs(-1), x))
    a_from_z(2)
    a_from_x(1)
    a_from_x(-1)
    b_from_z(1)
    a_from_z(3)
    a_from_x(2)
    a_from_x(-2)
    b_from_z(2)
    a_from_z(4)
    a_from_x(3)
    a_from_x(-3)
    b_from_z(3)
    a_from_x(4)
    for dz in range(NZ):
        a_relayed(dz)
    b_from_z(4)

    for d in range(NZ - 1):
        arrived(gains.at[pl.ds(zs(d + 1) * NX, NX)], gz_rsem.at[d])
    c_w.wait()

    inv = 1.0 / (COLS * (WIDE + NARROW))

    def total_step(c, carry):
        ta, tb = carry
        return ta + ga[c].astype(F32), tb + gb[c].astype(F32)

    zero = jnp.zeros((TOK, WIDE), F32), jnp.zeros((NARROW, WIDE), F32)

    def rows_of(ta, tb):
        low = jnp.sum(jnp.where(lane < NARROW, tb, 0.0), axis=1, keepdims=True)
        high = jnp.sum(jnp.where(lane < NARROW, 0.0, tb), axis=1, keepdims=True)
        return jnp.sum(ta, axis=1, keepdims=True) + jnp.concatenate([low, high], axis=0)

    def spread(v):
        wide = jnp.broadcast_to(v, (TOK, WIDE))
        return wide, jnp.where(lane < NARROW, wide[:NARROW], wide[NARROW:])

    mean = rows_of(*lax.fori_loop(0, COLS, total_step, zero)) * inv
    mean_a, mean_b = spread(mean)

    def var_step(c, carry):
        ta, tb = carry
        da, db = ga[c].astype(F32) - mean_a, gb[c].astype(F32) - mean_b
        return ta + da * da, tb + db * db

    var = rows_of(*lax.fori_loop(0, COLS, var_step, zero)) * inv
    rstd_a, rstd_b = spread(1.0 / jnp.sqrt(var + 1e-6))

    qk_v[...] = jnp.zeros_like(qk_v)

    @pl.loop(0, COLS // 2)
    def _(p):
        def normed(c):
            gg = gains[c]
            na = (ga[c].astype(F32) - mean_a) * rstd_a * gg[:, :WIDE]
            nb = (gb[c].astype(F32) - mean_b) * rstd_b * gg[:, WIDE:]
            return na.astype(BF16), nb

        a0, b0 = normed(2 * p)
        a1, b1 = normed(2 * p + 1)
        top = jnp.where(lane < NARROW, b0, pltpu.roll(b1, NARROW, 1))
        bottom = jnp.where(lane < NARROW, pltpu.roll(b0, NARROW, 1), b1)
        bb = jnp.concatenate([top, bottom], axis=0).astype(BF16)
        lhs = jnp.concatenate([a0, a1, bb], axis=1)
        w = w_v[p]
        rhs = jnp.concatenate([w[:128], w[192:320], w[128:192], w[320:384]], axis=0)
        qk_v[...] += jnp.dot(lhs, rhs, preferred_element_type=F32)

    qk_b = hid_v.at[0, pl.ds(0, TOK), pl.ds(0, qk_v.shape[1])]
    qk_b[...] = qk_v[...].astype(BF16)
    c_qk = pltpu.make_async_copy(qk_b, qk_out, out_sem.at[1])
    c_qk.start()
    for copy in sends:
        copy.wait_send()
    for k in range(2):
        @pl.when(core != k)
        def _():
            pltpu.make_async_copy(rs_send.at[6 + k], rs_send.at[6 + k], rs_ssem.at[6 + k]).wait()
    c_stream.wait()
    c_qk.wait()


def per_device(hidden, down_weight, residual, gain, qk_weight):
    depth, width = down_weight.shape
    full, heads = qk_weight.shape
    any_spec = pl.BlockSpec(memory_space=pl.ANY)
    dma = pltpu.SemaphoreType.DMA
    return pl.pallas_call(
        kernel,
        out_shape=(
            jax.ShapeDtypeStruct((TOK, width), BF16),
            jax.ShapeDtypeStruct((TOK, heads), BF16),
        ),
        in_specs=[any_spec] * 5,
        out_specs=(any_spec, any_spec),
        scratch_shapes=[
            pltpu.VMEM((NY, 2 * TOK, depth), BF16),
            pltpu.VMEM((depth, WIDE), BF16),
            pltpu.VMEM((depth, NARROW), BF16),
            pltpu.VMEM((depth, WIDE), BF16),
            pltpu.VMEM((TOK, width), BF16),
            pltpu.VMEM((1, width), BF16),
            pltpu.VMEM((COLS, 1, WIDE + 2 * NARROW), F32),
            pltpu.VMEM((COLS // 2, 2 * width, heads), BF16),
            pltpu.VMEM((TOK, width), BF16),
            pltpu.VMEM((TOK, heads), F32),
            pltpu.VMEM((ROWS, TOK + NARROW, WIDE), BF16),
            pltpu.VMEM((ROWS, TOK + NARROW, WIDE), BF16),
            pltpu.VMEM((COLS, TOK, WIDE), BF16),
            pltpu.VMEM((COLS, NARROW, WIDE), BF16),
            dma((9,)),
            dma((ROWS,)), dma((ROWS,)),
            dma((NX - 1,)), dma((NX - 1,)),
            dma((NZ - 1,)), dma((NZ - 1,)),
            dma((COLS,)), dma((2,)), dma((4,)), dma((NZ,)), dma((NZ + 1, 2)),
            dma((72,)), dma((2,)),
        ],
        compiler_params=pltpu.CompilerParams(
            collective_id=0, has_side_effects=True, vmem_limit_bytes=56 * 1024 * 1024
        ),
    )(hidden, down_weight, residual, gain.reshape(1, width), qk_weight.reshape(COLS // 2, 2 * width, heads))


def solution(mesh):
    placed = (P(None, "row"), P("row", "col"), P("row", "col"), P("col"), P(None, "col"))
    return jax.shard_map(
        per_device,
        mesh=mesh,
        in_specs=placed,
        out_specs=(P("row", "col"), P("row", "col")),
        check_vma=False,
    )
```

time: 215 us -> 54.5 us (0.25)
  waiting for transfers between devices: 108 us -> 0 us
  blocking collectives: 76.4 us -> 0 us
  Pallas kernels: 0 us -> 45.2 us
  between operations: 14.1 us -> 0.64 us
  matrix products: 9.47 us -> 0 us
  local copies, waits for them, and re-layouts: 3.17 us -> 8.38 us
  other arithmetic: 2.24 us -> 0 us
    all_gather x2 -> x0, blocking collectives: 76.4 us -> none  [joined(): pieces = jax.tree.map(lambda part: lax.all_gather(part, axis), value)]
    all_gather x1 -> x0, waiting for transfers between devices: 71.1 us -> none  [per_device(): lax.all_gather(normed, 'col', axis=1, tiled=True)]
    pallas_call x0 -> x1, Pallas kernels: none -> 45.2 us  [per_device(): pl.pallas_call(kernel, out_shape=(jax.ShapeDtypeStruct((TOK, width), BF16...]
    unnamed x3 -> x0, waiting for transfers between devices: 36.6 us -> none
    dot_general x2 -> x0, matrix products: 9.47 us -> none  [the longest x1 4.99 us: per_device(): jnp.dot(hidden, down_weight, preferred_element_type=jnp.float32)]
    unnamed x12 -> x3, local copies, waits for them, and re-layouts: 3.16 us -> 5.6 us
  transfers between devices with their start and end apart: 2 -> 0, of which waited for: 2 -> 0; matrix products, arithmetic and copies ran while one was open for 0% -> 0% of each run, Pallas kernels for 0% -> 0%
where the time goes in v1:
time: 54.5 us; the launch traced here: 54.3 us
  Pallas kernels  45.2 us (83%)
  local copies, waits for them, and re-layouts  8.38 us (15%)
  between operations  0.64 us (1%)
    pallas_call x1, Pallas kernels, per_device(): pl.pallas_call(kernel, out_shape=(jax.ShapeDtypeStruct((TOK, width), BF16...  45.2 us
    unnamed x3, local copies, waits for them, and re-layouts  5.6 us
    pallas_call x1, local copies, waits for them, and re-layouts, per_device(): pl.pallas_call(kernel, out_shape=(jax.ShapeDtypeStruct((TOK, width), BF16...  1.56 us
    reshape x1, local copies, waits for them, and re-layouts, per_device(): gain.reshape(1, width)  1.22 us

profile of v1, /device:TPU:2, one launch (start us, length us, event | category | flops | bytes accessed | tf_op | source)
XLA Modules:
  0.0 54.3 jit_solution(4343911620744470168)
XLA Ops:
  0.6 1.2 %reshape.10.gain = bf16[1,192]{1,0:T(2,128)(2,1)} reshape(bf16[192]{0:T(256)(128)(2,1)} %param.8) | data formatting | bytes 768 | tf_op jit(solution)/shard_map/reshape | solution.py:352
  1.8 1.5 %copy.8.residual = bf16[128,192]{1,0:T(8,128)(2,1)} copy(bf16[128,192]{0,1:T(8,128)(2,1)} %param.7) | data formatting | bytes 98304 | tf_op args[2]
  3.4 2.5 %copy.7.down = bf16[3072,192]{1,0:T(8,128)(2,1)} copy(bf16[3072,192]{0,1:T(8,128)(2,1)} %param.6) | data formatting | bytes 2359296 | tf_op args[1]
  5.9 45.2 %shard_map.68 = (bf16[128,192]{1,0:T(8,128)(2,1)}, bf16[128,384]{1,0:T(8,128)(2,1)}) custom-call(bf16[1024,3072]{1,0:T(8,128)(2,1)} %hidden.1, bf16[3072,192]{1,0:T(8,128)(2,1)} %copy.7.down, bf16[128,192]{1,0:T(8,128)(2,1)} %copy.8.residual, bf16[1,192]{1,0:T(2,128)(2,1)} %reshape.10.gain, bf16[16,384,384]{2,1,0:T(8,128)(2,1)} %bitcast.1), custom_call_target="tpu_custom_call" | custom-call | tf_op jit(solution)/shard_map/pallas_call | solution.py:319
  51.1 1.6 %copy.9 = bf16[128,192]{0,1:T(8,128)(2,1)} copy(bf16[128,192]{1,0:T(8,128)(2,1)} %get-tuple-element.2) | data formatting | bytes 98304 | tf_op jit(solution)/shard_map/pallas_call | solution.py:319
  52.7 1.5 %copy.11 = bf16[128,384]{1,0:T(8,128)(2,1)} copy(bf16[128,384]{1,0:T(8,128)(2,1)} %get-tuple-element.7) | data formatting | bytes 196608

commit v2 on v0

v2 whole, which is shorter than its diff:
```python
import functools

import jax
import jax.numpy as jnp
from jax import lax
from jax.experimental import pallas as pl
from jax.experimental.pallas import tpu as pltpu
from jax.sharding import PartitionSpec as P

MESH = pl.DeviceIdType.MESH
F32, BF16 = jnp.float32, jnp.bfloat16
NX, NZ, NY = 4, 8, 4
ROWS, COLS = 2 * NY, NZ * NX
TOK = 128
X_FIRST = 48
STEPS_Z = (1, -1, 2, -2, 3, -3, 4)
STEPS_X = (1, -1, 2)


def merge(stats, count):
    means, squares = stats[:, 0], stats[:, 1]
    mean = jnp.mean(means, axis=0, keepdims=True)
    off = means - mean
    square = jnp.sum(squares, axis=0, keepdims=True) + count * jnp.sum(off * off, axis=0, keepdims=True)
    return jnp.concatenate([mean, square], axis=0)


def kernel(
    hidden, down, residual, gain, weight, stream_out, qk_out,
    hid_v, down_v, res_v, gain_in, gains, gain_rows, w_v, qk_v, qk_b,
    rs_send, rs_recv, g, stats_z, stats_x,
    load_sem, rs_ssem, rs_rsem, gx_ssem, gx_rsem, gz_ssem, gz_rsem,
    sx_ssem, sx_rsem, sz_ssem, sz_rsem,
    a_rsem, bx_rsem, bz_rsem, ag_ssem, out_sem,
):
    row, col = lax.axis_index("row"), lax.axis_index("col")
    y, core = row // 2, row % 2
    z, x = col // NX, col % NX
    wide = down.shape[0]

    def at(zz, xx):
        return (row, zz * NX + xx)

    def zs(d):
        return lax.rem(z + d + NZ, NZ)

    def xs(d):
        return lax.rem(x + d + NX, NX)

    def load(src, dst, sem):
        copy = pltpu.make_async_copy(src, dst, load_sem.at[sem])
        copy.start()
        return copy

    c_gain = load(gain, gain_in, 6)
    c_down = load(down, down_v, 0)
    c_hid = []
    order = (2, 1, 3, 0)
    for i, d in enumerate(order):
        rows = pl.ds(pl.multiple_of(lax.rem(y + d, NY) * 2 * TOK, 2 * TOK), 2 * TOK)
        c_hid.append(load(hidden.at[rows], hid_v.at[i], 2 + i))
    c_res = load(residual, res_v, 7)

    barrier = pltpu.get_barrier_semaphore()
    peers = [(lax.rem(row + d, ROWS), col) for d in range(1, ROWS)]
    peers += [at(z, xs(d)) for d in STEPS_X]
    peers += [at(zs(d), x) for d in STEPS_Z]
    for peer in peers:
        pl.semaphore_signal(barrier, inc=1, device_id=peer, device_id_type=MESH)

    c_gain.wait()
    gains[col] = gain_in[...].astype(F32)
    pl.semaphore_wait(barrier, len(peers))

    sends = []

    def send(src, dst, ssem, rsem, peer):
        copy = pltpu.make_async_remote_copy(
            src_ref=src, dst_ref=dst, send_sem=ssem, recv_sem=rsem,
            device_id=peer, device_id_type=MESH,
        )
        copy.start()
        return copy

    def arrived(ref, rsem):
        pltpu.make_async_copy(ref, ref, rsem).wait()

    def over_x(ref, ssem, rsem):
        for i, d in enumerate(STEPS_X):
            sends.append(send(ref, ref, ssem.at[i], rsem.at[x], at(z, xs(d))))

    def over_z(ref, ssem, rsem):
        for i, d in enumerate(STEPS_Z):
            sends.append(send(ref, ref, ssem.at[i], rsem.at[z], at(zs(d), x)))

    over_x(gains.at[col], gx_ssem, gx_rsem)

    c_down.wait()
    for i, d in enumerate(order):
        c_hid[i].wait()
        part = lax.dot_general(
            down_v[...], hid_v[i], (((1,), (1,)), ((), ())), preferred_element_type=F32
        ).astype(BF16)
        yy = lax.rem(y + d, NY)
        for k in range(2):
            rs_send[2 * i + k] = part[:, k * TOK:(k + 1) * TOK]
        for k in range(2):
            peer = (yy * 2 + k, col)
            if d:
                sends.append(send(rs_send.at[2 * i + k], rs_recv.at[row], rs_ssem.at[2 * i + k], rs_rsem.at[row], peer))
            else:
                @pl.when(core != k)
                def _():
                    send(rs_send.at[2 * i + k], rs_recv.at[row], rs_ssem.at[2 * i + k], rs_rsem.at[row], peer)

                @pl.when(core == k)
                def _():
                    rs_recv[row] = rs_send[2 * i + k]

    c_w = load(weight, w_v, 8)

    for d in STEPS_X:
        arrived(gains.at[z * NX + xs(d)], gx_rsem.at[xs(d)])
    over_z(gains.at[pl.ds(z * NX, NX)], gz_ssem, gz_rsem)

    for d in range(1, ROWS):
        r = lax.rem(row + d, ROWS)
        arrived(rs_recv.at[r], rs_rsem.at[r])
    c_res.wait()
    total = rs_recv[0].astype(F32)
    for r in range(1, ROWS):
        total = total + rs_recv[r].astype(F32)
    stream = (res_v[...].astype(F32) + total).astype(BF16)
    g[col] = stream

    last = pl.ds(X_FIRST, wide - X_FIRST)
    first = pl.ds(0, X_FIRST)
    count = [0]

    def push(ref, rsem, peer):
        sends.append(send(ref, ref, ag_ssem.at[count[0]], rsem, peer))
        count[0] += 1

    def push_x(dz):
        slot = zs(dz) * NX + x
        for e in STEPS_X:
            push(g.at[slot, last], a_rsem.at[slot], at(z, xs(e)))

    def group(dz):
        return g.at[pl.ds(zs(dz) * NX, NX), first]

    for e in STEPS_X:
        push(g.at[col, first], bx_rsem.at[x], at(z, xs(e)))
    for d in STEPS_Z:
        push(g.at[col, last], a_rsem.at[col], at(zs(d), x))

    values = stream.astype(F32)
    mean = jnp.mean(values, axis=0, keepdims=True)
    off = values - mean
    stats_z[z] = jnp.concatenate([mean, jnp.sum(off * off, axis=0, keepdims=True)], axis=0)
    over_z(stats_z.at[z], sz_ssem, sz_rsem)
    push_x(0)
    c_stream = pltpu.make_async_copy(g.at[col], stream_out, out_sem.at[0])
    c_stream.start()

    for e in STEPS_X:
        arrived(g.at[z * NX + xs(e), first], bx_rsem.at[xs(e)])
    for d in (4, 3, -3, 2, -2, 1, -1):
        push(group(0), bz_rsem.at[z], at(zs(d), x))

    for d in STEPS_Z:
        arrived(gains.at[pl.ds(zs(d) * NX, NX)], gz_rsem.at[zs(d)])
    for c in range(NZ):
        gain_rows[c] = jnp.concatenate([gains[c * NX + k] for k in range(NX)], axis=1)

    def from_z(d):
        slot = zs(d) * NX + x
        arrived(g.at[slot, last], a_rsem.at[slot])
        push_x(d)

    for d in STEPS_Z[:4]:
        from_z(d)
    for d in STEPS_Z:
        arrived(stats_z.at[zs(d)], sz_rsem.at[zs(d)])
    stats_x[x] = merge(stats_z[...], wide)
    over_x(stats_x.at[x], sx_ssem, sx_rsem)
    for d in STEPS_Z[4:]:
        from_z(d)

    for e in STEPS_X:
        arrived(stats_x.at[xs(e)], sx_rsem.at[xs(e)])
    both = merge(stats_x[...], NZ * wide)
    scale = 1.0 / jnp.sqrt(both[1:] * (1.0 / (COLS * wide)) + 1e-6)
    mean_t = jnp.transpose(jnp.broadcast_to(both[:1], (TOK, TOK)))
    scale_t = jnp.transpose(jnp.broadcast_to(scale, (TOK, TOK)))
    c_w.wait()

    for i, d in enumerate((0,) + STEPS_Z):
        for e in STEPS_X:
            slot = zs(d) * NX + xs(e)
            arrived(g.at[slot, last], a_rsem.at[slot])
        if d:
            arrived(group(d), bz_rsem.at[zs(d)])
        zz = zs(d)
        block = g[pl.ds(zz * NX, NX)].reshape(NX * wide, TOK)
        tokens = jnp.transpose(block)
        row_gain = gain_rows[zz]
        pieces = []
        for k in range(NX * wide // TOK):
            lanes = slice(k * TOK, (k + 1) * TOK)
            piece = (tokens[:, lanes].astype(F32) - mean_t) * scale_t * row_gain[:, lanes]
            pieces.append(piece.astype(BF16))
        out = jnp.dot(jnp.concatenate(pieces, axis=1), w_v[zz], preferred_element_type=F32)
        if i == 0:
            qk_v[...] = out
        elif i < NZ - 1:
            qk_v[...] += out
        else:
            qk_b[...] = (qk_v[...] + out).astype(BF16)

    c_qk = pltpu.make_async_copy(qk_b, qk_out, out_sem.at[1])
    c_qk.start()
    for copy in sends:
        copy.wait_send()
    for k in range(2):
        @pl.when(core != k)
        def _():
            pltpu.make_async_copy(rs_send.at[6 + k], rs_send.at[6 + k], rs_ssem.at[6 + k]).wait()
    c_stream.wait()
    c_qk.wait()


def per_device(hidden, down_weight, residual, gain, qk_weight):
    depth, width = down_weight.shape
    full, heads = qk_weight.shape
    any_spec = pl.BlockSpec(memory_space=pl.ANY)
    dma = pltpu.SemaphoreType.DMA
    stream, queries_keys = pl.pallas_call(
        kernel,
        out_shape=(
            jax.ShapeDtypeStruct((width, TOK), BF16),
            jax.ShapeDtypeStruct((TOK, heads), BF16),
        ),
        in_specs=[any_spec] * 5,
        out_specs=(any_spec, any_spec),
        scratch_shapes=[
            pltpu.VMEM((NY, 2 * TOK, depth), BF16),
            pltpu.VMEM((width, depth), BF16),
            pltpu.VMEM((width, TOK), BF16),
            pltpu.VMEM((1, width), BF16),
            pltpu.VMEM((COLS, 1, width), F32),
            pltpu.VMEM((NZ, 1, NX * width), F32),
            pltpu.VMEM((NZ, NX * width, heads), BF16),
            pltpu.VMEM((TOK, heads), F32),
            pltpu.VMEM((TOK, heads), BF16),
            pltpu.VMEM((ROWS, width, TOK), BF16),
            pltpu.VMEM((ROWS, width, TOK), BF16),
            pltpu.VMEM((COLS, width, TOK), BF16),
            pltpu.VMEM((NZ, 2, TOK), F32),
            pltpu.VMEM((NX, 2, TOK), F32),
            dma((9,)),
            dma((ROWS,)), dma((ROWS,)),
            dma((NX - 1,)), dma((NX,)), dma((NZ - 1,)), dma((NZ,)),
            dma((NX - 1,)), dma((NX,)), dma((NZ - 1,)), dma((NZ,)),
            dma((COLS,)), dma((NX,)), dma((NZ,)),
            dma((48,)), dma((2,)),
        ],
        compiler_params=pltpu.CompilerParams(
            collective_id=0, has_side_effects=True, vmem_limit_bytes=56 * 1024 * 1024
        ),
    )(
        hidden, down_weight.T, residual.T, gain.reshape(1, width),
        qk_weight.reshape(NZ, NX * width, heads),
    )
    return stream.T, queries_keys


def solution(mesh):
    placed = (P(None, "row"), P("row", "col"), P("row", "col"), P("col"), P(None, "col"))
    return jax.shard_map(
        per_device,
        mesh=mesh,
        in_specs=placed,
        out_specs=(P("row", "col"), P("row", "col")),
        check_vma=False,
    )
```

time: 215 us -> 44 us (0.20)
  the two profiles are of different devices: /device:TPU:2 before, /device:TPU:1 now
where the time goes in v2:
time: 44 us; the launch traced here: 43.8 us
  Pallas kernels  39 us (89%)
  local copies, waits for them, and re-layouts  4.18 us (10%)
  between operations  0.64 us (1%)
    pallas_call x1, Pallas kernels, per_device(): pl.pallas_call(kernel, out_shape=(jax.ShapeDtypeStruct((width, TOK), BF16...  39 us
    unnamed x2, local copies, waits for them, and re-layouts  2.96 us
    reshape x1, local copies, waits for them, and re-layouts, per_device(): gain.reshape(1, width)  1.22 us

profile of v2, /device:TPU:1, one launch (start us, length us, event | category | flops | bytes accessed | tf_op | source)
XLA Modules:
  0.0 43.8 jit_solution(9220996417472627528)
XLA Ops:
  0.6 1.2 %reshape.10.gain = bf16[1,192]{1,0:T(2,128)(2,1)} reshape(bf16[192]{0:T(256)(128)(2,1)} %param.8) | data formatting | bytes 768 | tf_op jit(solution)/shard_map/reshape | solution.py:272
  1.8 39.0 %shard_map.68 = (bf16[192,128]{1,0:T(8,128)(2,1)}, bf16[128,384]{1,0:T(8,128)(2,1)}) custom-call(bf16[1024,3072]{1,0:T(8,128)(2,1)} %hidden.1, bf16[192,3072]{1,0:T(8,128)(2,1)} %bitcast.5, bf16[192,128]{1,0:T(8,128)(2,1)} %bitcast.6, bf16[1,192]{1,0:T(2,128)(2,1)} %reshape.10.gain, bf16[8,768,384]{2,1,0:T(8,128)(2,1)} %bitcast.4), custom_call_target="tpu_custom_call" | custom-call | tf_op jit(solution)/shard_map/pallas_call | solution.py:238
  40.8 1.4 %copy.9 = bf16[128,192]{0,1:T(8,128)(2,1)} copy(bf16[128,192]{0,1:T(8,128)(2,1)} %bitcast.7) | data formatting | bytes 98304
  42.3 1.5 %copy.10 = bf16[128,384]{1,0:T(8,128)(2,1)} copy(bf16[128,384]{1,0:T(8,128)(2,1)} %get-tuple-element.9) | data formatting | bytes 196608

commit v3 on v2

--- a/solution.py
+++ b/solution.py
@@ -27,11 +27,11 @@
 
 def kernel(
     hidden, down, residual, gain, weight, stream_out, qk_out,
-    hid_v, down_v, res_v, gain_in, gains, gain_rows, w_v, qk_v, qk_b,
+    hid_v, down_v, res_v, gain_in, gains, gain_rows, w_v, qk_v,
     rs_send, rs_recv, g, stats_z, stats_x,
     load_sem, rs_ssem, rs_rsem, gx_ssem, gx_rsem, gz_ssem, gz_rsem,
     sx_ssem, sx_rsem, sz_ssem, sz_rsem,
-    a_rsem, bx_rsem, bz_rsem, ag_ssem, out_sem,
+    a_rsem, bx_rsem, bz_rsem, ag_ssem,
 ):
     row, col = lax.axis_index("row"), lax.axis_index("col")
     y, core = row // 2, row % 2
@@ -68,10 +68,6 @@
     for peer in peers:
         pl.semaphore_signal(barrier, inc=1, device_id=peer, device_id_type=MESH)
 
-    c_gain.wait()
-    gains[col] = gain_in[...].astype(F32)
-    pl.semaphore_wait(barrier, len(peers))
-
     sends = []
 
     def send(src, dst, ssem, rsem, peer):
@@ -93,35 +89,50 @@
         for i, d in enumerate(STEPS_Z):
             sends.append(send(ref, ref, ssem.at[i], rsem.at[z], at(zs(d), x)))
 
-    over_x(gains.at[col], gx_ssem, gx_rsem)
-
-    c_down.wait()
-    for i, d in enumerate(order):
+    def project(i):
         c_hid[i].wait()
         part = lax.dot_general(
             down_v[...], hid_v[i], (((1,), (1,)), ((), ())), preferred_element_type=F32
         ).astype(BF16)
-        yy = lax.rem(y + d, NY)
         for k in range(2):
             rs_send[2 * i + k] = part[:, k * TOK:(k + 1) * TOK]
+
+    def leave(i):
+        yy = lax.rem(y + order[i], NY)
         for k in range(2):
+            piece = rs_send.at[2 * i + k]
             peer = (yy * 2 + k, col)
-            if d:
-                sends.append(send(rs_send.at[2 * i + k], rs_recv.at[row], rs_ssem.at[2 * i + k], rs_rsem.at[row], peer))
+            if order[i]:
+                sends.append(send(piece, rs_recv.at[row], rs_ssem.at[2 * i + k], rs_rsem.at[row], peer))
             else:
                 @pl.when(core != k)
                 def _():
-                    send(rs_send.at[2 * i + k], rs_recv.at[row], rs_ssem.at[2 * i + k], rs_rsem.at[row], peer)
+                    send(piece, rs_recv.at[row], rs_ssem.at[2 * i + k], rs_rsem.at[row], peer)
 
                 @pl.when(core == k)
                 def _():
-                    rs_recv[row] = rs_send[2 * i + k]
+                    rs_recv[row] = piece[...]
+
+    c_down.wait()
+    project(0)
+    c_gain.wait()
+    gains[col] = gain_in[...].astype(F32).reshape(1, wide)
+    pl.semaphore_wait(barrier, len(peers))
+    leave(0)
+    over_x(gains.at[col], gx_ssem, gx_rsem)
+    for i in range(1, NY):
+        project(i)
+        leave(i)
 
     c_w = load(weight, w_v, 8)
 
     for d in STEPS_X:
         arrived(gains.at[z * NX + xs(d)], gx_rsem.at[xs(d)])
     over_z(gains.at[pl.ds(z * NX, NX)], gz_ssem, gz_rsem)
+    for d in STEPS_Z:
+        arrived(gains.at[pl.ds(zs(d) * NX, NX)], gz_rsem.at[zs(d)])
+    for c in range(NZ):
+        gain_rows[c] = jnp.concatenate([gains[c * NX + k] for k in range(NX)], axis=1)
 
     for d in range(1, ROWS):
         r = lax.rem(row + d, ROWS)
@@ -154,24 +165,19 @@
     for d in STEPS_Z:
         push(g.at[col, last], a_rsem.at[col], at(zs(d), x))
 
+    push_x(0)
+
     values = stream.astype(F32)
     mean = jnp.mean(values, axis=0, keepdims=True)
     off = values - mean
     stats_z[z] = jnp.concatenate([mean, jnp.sum(off * off, axis=0, keepdims=True)], axis=0)
     over_z(stats_z.at[z], sz_ssem, sz_rsem)
-    push_x(0)
-    c_stream = pltpu.make_async_copy(g.at[col], stream_out, out_sem.at[0])
-    c_stream.start()
+    stream_out[...] = stream
 
     for e in STEPS_X:
         arrived(g.at[z * NX + xs(e), first], bx_rsem.at[xs(e)])
     for d in (4, 3, -3, 2, -2, 1, -1):
         push(group(0), bz_rsem.at[z], at(zs(d), x))
-
-    for d in STEPS_Z:
-        arrived(gains.at[pl.ds(zs(d) * NX, NX)], gz_rsem.at[zs(d)])
-    for c in range(NZ):
-        gain_rows[c] = jnp.concatenate([gains[c * NX + k] for k in range(NX)], axis=1)
 
     def from_z(d):
         slot = zs(d) * NX + x
@@ -216,43 +222,47 @@
         elif i < NZ - 1:
             qk_v[...] += out
         else:
-            qk_b[...] = (qk_v[...] + out).astype(BF16)
-
-    c_qk = pltpu.make_async_copy(qk_b, qk_out, out_sem.at[1])
-    c_qk.start()
+            qk_out[...] = (qk_v[...] + out).astype(BF16)
+
     for copy in sends:
         copy.wait_send()
     for k in range(2):
         @pl.when(core != k)
         def _():
             pltpu.make_async_copy(rs_send.at[6 + k], rs_send.at[6 + k], rs_ssem.at[6 + k]).wait()
-    c_stream.wait()
-    c_qk.wait()
+
+
+def deliver(stream, queries_keys, stream_out, qk_out, sem):
+    copies = [
+        pltpu.make_async_copy(stream, stream_out, sem.at[0]),
+        pltpu.make_async_copy(queries_keys, qk_out, sem.at[1]),
+    ]
+    for copy in copies:
+        copy.start()
+    for copy in copies:
+        copy.wait()
 
 
 def per_device(hidden, down_weight, residual, gain, qk_weight):
     depth, width = down_weight.shape
     full, heads = qk_weight.shape
+    vmem_spec = pl.BlockSpec(memory_space=pltpu.VMEM)
     any_spec = pl.BlockSpec(memory_space=pl.ANY)
     dma = pltpu.SemaphoreType.DMA
     stream, queries_keys = pl.pallas_call(
         kernel,
-        out_shape=(
-            jax.ShapeDtypeStruct((width, TOK), BF16),
-            jax.ShapeDtypeStruct((TOK, heads), BF16),
-        ),
+        out_shape=(pltpu.VMEM((width, TOK), BF16), pltpu.VMEM((TOK, heads), BF16)),
         in_specs=[any_spec] * 5,
-        out_specs=(any_spec, any_spec),
+        out_specs=(vmem_spec, vmem_spec),
         scratch_shapes=[
             pltpu.VMEM((NY, 2 * TOK, depth), BF16),
             pltpu.VMEM((width, depth), BF16),
             pltpu.VMEM((width, TOK), BF16),
-            pltpu.VMEM((1, width), BF16),
+            pltpu.VMEM((width,), BF16),
             pltpu.VMEM((COLS, 1, width), F32),
             pltpu.VMEM((NZ, 1, NX * width), F32),
             pltpu.VMEM((NZ, NX * width, heads), BF16),
             pltpu.VMEM((TOK, heads), F32),
-            pltpu.VMEM((TOK, heads), BF16),
             pltpu.VMEM((ROWS, width, TOK), BF16),
             pltpu.VMEM((ROWS, width, TOK), BF16),
             pltpu.VMEM((COLS, width, TOK), BF16),
@@ -263,14 +273,27 @@
             dma((NX - 1,)), dma((NX,)), dma((NZ - 1,)), dma((NZ,)),
             dma((NX - 1,)), dma((NX,)), dma((NZ - 1,)), dma((NZ,)),
             dma((COLS,)), dma((NX,)), dma((NZ,)),
-            dma((48,)), dma((2,)),
+            dma((48,)),
         ],
         compiler_params=pltpu.CompilerParams(
             collective_id=0, has_side_effects=True, vmem_limit_bytes=56 * 1024 * 1024
         ),
     )(
-        hidden, down_weight.T, residual.T, gain.reshape(1, width),
+        hidden, down_weight.T, residual.T, gain,
         qk_weight.reshape(NZ, NX * width, heads),
+    )
+    stream, queries_keys = pl.pallas_call(
+        deliver,
+        out_shape=(
+            jax.ShapeDtypeStruct((width, TOK), BF16),
+            jax.ShapeDtypeStruct((TOK, heads), BF16),
+        ),
+        in_specs=[vmem_spec] * 2,
+        out_specs=(any_spec, any_spec),
+        scratch_shapes=[dma((2,))],
+    )(
+        pltpu.with_memory_space_constraint(stream, pltpu.VMEM),
+        pltpu.with_memory_space_constraint(queries_keys, pltpu.VMEM),
     )
     return stream.T, queries_keys
 

time: 44 us -> 38.6 us (0.88)
  the two profiles are of different devices: /device:TPU:1 before, /device:TPU:2 now
where the time goes in v3:
time: 38.6 us; the launch traced here: 38.5 us
  Pallas kernels  37.9 us (98%)
  between operations  0.64 us (2%)
    pallas_call x1, Pallas kernels, per_device(): pl.pallas_call(kernel, out_shape=(pltpu.VMEM((width, TOK), BF16), pltpu.V...  37.2 us

profile of v3, /device:TPU:2, one launch (start us, length us, event | category | flops | bytes accessed | tf_op | source)
XLA Modules:
  0.0 38.5 jit_solution(17130771587232059206)
XLA Ops:
  0.6 37.2 %shard_map.68 = (bf16[192,128]{1,0:T(8,128)(2,1)S(1)}, bf16[128,384]{1,0:T(8,128)(2,1)S(1)}) custom-call(bf16[1024,3072]{1,0:T(8,128)(2,1)} %hidden.1, bf16[192,3072]{1,0:T(8,128)(2,1)} %bitcast.5, bf16[192,128]{1,0:T(8,128)(2,1)} %bitcast.6, bf16[192]{0:T(256)(128)(2,1)} %gain.1, bf16[8,768,384]{2,1,0:T(8,128)(2,1)} %bitcast.4), custom_call_target="tpu_custom_call" | custom-call | tf_op jit(solution)/shard_map/pallas_call | solution.py:252
  37.9 0.7 %shard_map.69 = (bf16[192,128]{1,0:T(8,128)(2,1)}, bf16[128,384]{1,0:T(8,128)(2,1)}) custom-call(bf16[192,128]{1,0:T(8,128)(2,1)S(1)} %get-tuple-element.6.stream, bf16[128,384]{1,0:T(8,128)(2,1)S(1)} %get-tuple-element.7.queries_keys), custom_call_target="tpu_custom_call" | custom-call | tf_op jit(solution)/shard_map/pallas_call | solution.py:285

commit v4 on v3

--- a/solution.py
+++ b/solution.py
@@ -28,8 +28,8 @@
 def kernel(
     hidden, down, residual, gain, weight, stream_out, qk_out,
     hid_v, down_v, res_v, gain_in, gains, gain_rows, w_v, qk_v,
-    rs_send, rs_recv, g, stats_z, stats_x,
-    load_sem, rs_ssem, rs_rsem, gx_ssem, gx_rsem, gz_ssem, gz_rsem,
+    pair_send, pair_recv, rs_send, rs_recv, g, stats_z, stats_x,
+    load_sem, pair_ssem, pair_rsem, rs_ssem, rs_rsem, gx_ssem, gx_rsem, gz_ssem, gz_rsem,
     sx_ssem, sx_rsem, sz_ssem, sz_rsem,
     a_rsem, bx_rsem, bz_rsem, ag_ssem,
 ):
@@ -52,17 +52,25 @@
         copy.start()
         return copy
 
-    c_gain = load(gain, gain_in, 6)
+    order = (2, 1), (3, 0)
+    parts = [(1 - core, order[0]), (1 - core, order[1]), (core, order[0]), (core, order[1])]
+
+    def load_hidden(i):
+        owner, places = parts[i]
+        copies = []
+        for k, d in enumerate(places):
+            first_row = (lax.rem(y + d, NY) * 2 + owner) * TOK
+            rows = pl.ds(pl.multiple_of(first_row, TOK), TOK)
+            copies.append(load(hidden.at[rows], hid_v.at[i, pl.ds(k * TOK, TOK)], 8 + 2 * i + k))
+        return copies
+
+    c_gain = load(gain, gain_in, 1)
     c_down = load(down, down_v, 0)
-    c_hid = []
-    order = (2, 1, 3, 0)
-    for i, d in enumerate(order):
-        rows = pl.ds(pl.multiple_of(lax.rem(y + d, NY) * 2 * TOK, 2 * TOK), 2 * TOK)
-        c_hid.append(load(hidden.at[rows], hid_v.at[i], 2 + i))
-    c_res = load(residual, res_v, 7)
+    c_hid = [load_hidden(0)]
 
     barrier = pltpu.get_barrier_semaphore()
-    peers = [(lax.rem(row + d, ROWS), col) for d in range(1, ROWS)]
+    sibling = (y * 2 + 1 - core, col)
+    peers = [sibling] + [(lax.rem(y + d, NY) * 2 + core, col) for d in range(1, NY)]
     peers += [at(z, xs(d)) for d in STEPS_X]
     peers += [at(zs(d), x) for d in STEPS_Z]
     for peer in peers:
@@ -90,58 +98,60 @@
             sends.append(send(ref, ref, ssem.at[i], rsem.at[z], at(zs(d), x)))
 
     def project(i):
-        c_hid[i].wait()
-        part = lax.dot_general(
+        for copy in c_hid[i]:
+            copy.wait()
+        if i + 2 < NY:
+            c_hid.append(load_hidden(i + 2))
+        return lax.dot_general(
             down_v[...], hid_v[i], (((1,), (1,)), ((), ())), preferred_element_type=F32
-        ).astype(BF16)
+        )
+
+    def to_sibling(i):
         for k in range(2):
-            rs_send[2 * i + k] = part[:, k * TOK:(k + 1) * TOK]
-
-    def leave(i):
-        yy = lax.rem(y + order[i], NY)
+            j = 2 * i + k
+            sends.append(send(pair_send.at[j], pair_recv.at[j], pair_ssem.at[j], pair_rsem.at[j], sibling))
+
+    def hand(i):
+        part = project(i).astype(BF16)
         for k in range(2):
-            piece = rs_send.at[2 * i + k]
-            peer = (yy * 2 + k, col)
-            if order[i]:
-                sends.append(send(piece, rs_recv.at[row], rs_ssem.at[2 * i + k], rs_rsem.at[row], peer))
-            else:
-                @pl.when(core != k)
-                def _():
-                    send(piece, rs_recv.at[row], rs_ssem.at[2 * i + k], rs_rsem.at[row], peer)
-
-                @pl.when(core == k)
-                def _():
-                    rs_recv[row] = piece[...]
+            pair_send[2 * i + k] = part[:, k * TOK:(k + 1) * TOK]
 
     c_down.wait()
-    project(0)
+    c_hid.append(load_hidden(1))
+    hand(0)
     c_gain.wait()
     gains[col] = gain_in[...].astype(F32).reshape(1, wide)
     pl.semaphore_wait(barrier, len(peers))
-    leave(0)
+    to_sibling(0)
     over_x(gains.at[col], gx_ssem, gx_rsem)
-    for i in range(1, NY):
-        project(i)
-        leave(i)
-
-    c_w = load(weight, w_v, 8)
+    hand(1)
+    to_sibling(1)
+    c_res = load(residual, res_v, 2)
+    own = None
+    for i in range(2):
+        part = project(2 + i)
+        for k in range(2):
+            j, d = 2 * i + k, order[i][k]
+            arrived(pair_recv.at[j], pair_rsem.at[j])
+            both = part[:, k * TOK:(k + 1) * TOK] + pair_recv[j].astype(F32)
+            if d:
+                rs_send[d - 1] = both.astype(BF16)
+                peer = (lax.rem(y + d, NY) * 2 + core, col)
+                sends.append(send(rs_send.at[d - 1], rs_recv.at[NY - 1 - d], rs_ssem.at[d - 1], rs_rsem.at[NY - 1 - d], peer))
+            else:
+                own = both
+
+    c_w = load(weight, w_v, 3)
 
     for d in STEPS_X:
         arrived(gains.at[z * NX + xs(d)], gx_rsem.at[xs(d)])
     over_z(gains.at[pl.ds(z * NX, NX)], gz_ssem, gz_rsem)
-    for d in STEPS_Z:
-        arrived(gains.at[pl.ds(zs(d) * NX, NX)], gz_rsem.at[zs(d)])
-    for c in range(NZ):
-        gain_rows[c] = jnp.concatenate([gains[c * NX + k] for k in range(NX)], axis=1)
-
-    for d in range(1, ROWS):
-        r = lax.rem(row + d, ROWS)
-        arrived(rs_recv.at[r], rs_rsem.at[r])
     c_res.wait()
-    total = rs_recv[0].astype(F32)
-    for r in range(1, ROWS):
-        total = total + rs_recv[r].astype(F32)
-    stream = (res_v[...].astype(F32) + total).astype(BF16)
+    total = res_v[...].astype(F32) + own
+    for d in range(NY - 1):
+        arrived(rs_recv.at[d], rs_rsem.at[d])
+        total = total + rs_recv[d].astype(F32)
+    stream = total.astype(BF16)
     g[col] = stream
 
     last = pl.ds(X_FIRST, wide - X_FIRST)
@@ -192,6 +202,11 @@
     over_x(stats_x.at[x], sx_ssem, sx_rsem)
     for d in STEPS_Z[4:]:
         from_z(d)
+
+    for d in STEPS_Z:
+        arrived(gains.at[pl.ds(zs(d) * NX, NX)], gz_rsem.at[zs(d)])
+    for c in range(NZ):
+        gain_rows[c] = jnp.concatenate([gains[c * NX + k] for k in range(NX)], axis=1)
 
     for e in STEPS_X:
         arrived(stats_x.at[xs(e)], sx_rsem.at[xs(e)])
@@ -226,10 +241,6 @@
 
     for copy in sends:
         copy.wait_send()
-    for k in range(2):
-        @pl.when(core != k)
-        def _():
-            pltpu.make_async_copy(rs_send.at[6 + k], rs_send.at[6 + k], rs_ssem.at[6 + k]).wait()
 
 
 def deliver(stream, queries_keys, stream_out, qk_out, sem):
@@ -263,13 +274,15 @@
             pltpu.VMEM((NZ, 1, NX * width), F32),
             pltpu.VMEM((NZ, NX * width, heads), BF16),
             pltpu.VMEM((TOK, heads), F32),
-            pltpu.VMEM((ROWS, width, TOK), BF16),
-            pltpu.VMEM((ROWS, width, TOK), BF16),
+            pltpu.VMEM((NY, width, TOK), BF16),
+            pltpu.VMEM((NY, width, TOK), BF16),
+            pltpu.VMEM((NY - 1, width, TOK), BF16),
+            pltpu.VMEM((NY - 1, width, TOK), BF16),
             pltpu.VMEM((COLS, width, TOK), BF16),
             pltpu.VMEM((NZ, 2, TOK), F32),
             pltpu.VMEM((NX, 2, TOK), F32),
-            dma((9,)),
-            dma((ROWS,)), dma((ROWS,)),
+            dma((16,)),
+            dma((NY,)), dma((NY,)), dma((NY - 1,)), dma((NY - 1,)),
             dma((NX - 1,)), dma((NX,)), dma((NZ - 1,)), dma((NZ,)),
             dma((NX - 1,)), dma((NX,)), dma((NZ - 1,)), dma((NZ,)),
             dma((COLS,)), dma((NX,)), dma((NZ,)),

time: 38.6 us -> 37.1 us (0.961)
  Pallas kernels: 37.9 us -> 36.3 us
    pallas_call x1, Pallas kernels: 37.2 us -> 35.6 us  [per_device(): pl.pallas_call(kernel, out_shape=(pltpu.VMEM((width, TOK), BF16), pltpu.V...]
where the time goes in v4:
time: 37.1 us; the launch traced here: 37 us
  Pallas kernels  36.3 us (98%)
  between operations  0.64 us (2%)
    pallas_call x1, Pallas kernels, per_device(): pl.pallas_call(kernel, out_shape=(pltpu.VMEM((width, TOK), BF16), pltpu.V...  35.6 us

profile of v4, /device:TPU:2, one launch (start us, length us, event | category | flops | bytes accessed | tf_op | source)
XLA Modules:
  0.0 37.0 jit_solution(4991064052353762760)
XLA Ops:
  0.6 35.6 %shard_map.68 = (bf16[192,128]{1,0:T(8,128)(2,1)S(1)}, bf16[128,384]{1,0:T(8,128)(2,1)S(1)}) custom-call(bf16[1024,3072]{1,0:T(8,128)(2,1)} %hidden.1, bf16[192,3072]{1,0:T(8,128)(2,1)} %bitcast.5, bf16[192,128]{1,0:T(8,128)(2,1)} %bitcast.6, bf16[192]{0:T(256)(128)(2,1)} %gain.1, bf16[8,768,384]{2,1,0:T(8,128)(2,1)} %bitcast.4), custom_call_target="tpu_custom_call" | custom-call | tf_op jit(solution)/shard_map/pallas_call | solution.py:263
  36.3 0.7 %shard_map.69 = (bf16[192,128]{1,0:T(8,128)(2,1)}, bf16[128,384]{1,0:T(8,128)(2,1)}) custom-call(bf16[192,128]{1,0:T(8,128)(2,1)S(1)} %get-tuple-element.6.stream, bf16[128,384]{1,0:T(8,128)(2,1)S(1)} %get-tuple-element.7.queries_keys), custom_call_target="tpu_custom_call" | custom-call | tf_op jit(solution)/shard_map/pallas_call | solution.py:298

commit v5 on v4

--- a/solution.py
+++ b/solution.py
@@ -16,6 +16,26 @@
 STEPS_Z = (1, -1, 2, -2, 3, -3, 4)
 STEPS_X = (1, -1, 2)
 
+SHARE_AT = 12
+MERGE_AT = ("z", -3)
+ORDER = (
+    ("s", "z", 1), ("s", "z", -1), ("s", "bx", 2), ("s", "x", 0, -1), ("s", "bx", -1), ("s", "z", 2), ("s", "z", 3),
+    ("s", "bx", 1), ("s", "z", -3), ("s", "z", -2), ("s", "x", 0, 2), ("s", "x", 0, 1), ("w", "z", 1),
+    ("s", "x", 1, 2), ("w", "z", -1), ("w", "bx", 1), ("s", "x", 1, -1), ("s", "x", 1, 1), ("s", "x", -1, 2),
+    ("s", "x", -1, -1), ("w", "bx", 2), ("w", "bx", -1), ("s", "bz", -3), ("s", "bz", 3), ("s", "bz", -1),
+    ("s", "x", -1, 1), ("s", "bz", 1), ("w", "z", 2), ("s", "x", 2, 2), ("s", "x", 2, 1), ("s", "x", 2, -1),
+    ("w", "z", 3), ("s", "x", 3, 1), ("w", "z", -3), ("s", "z4", 3), ("s", "x", -3, -1), ("w", "z", -2),
+    ("s", "z4", -3), ("s", "bz", 2), ("s", "bz", -2), ("s", "x", 3, 2), ("s", "x", -2, 1), ("s", "x", -2, -1),
+    ("s", "bz", 4), ("w", "x", -1, 2), ("s", "x", -3, 2), ("w", "x", 1, -1), ("w", "bz", -1), ("s", "x", -3, 1),
+    ("s", "x", 3, -1), ("w", "bz", 1), ("s", "x", -2, 2), ("w", "x", 0, 1), ("w", "x", -1, -1), ("w", "bz", -3),
+    ("w", "x", 2, 1), ("w", "x", 0, -1), ("w", "x", 1, 1), ("w", "z4", 3), ("w", "x", -3, -1), ("w", "x", 3, 1),
+    ("w", "x", 2, 2), ("w", "z4", -3), ("w", "bz", 3), ("s", "x", 4, 2), ("w", "x", 0, 2), ("c", 0),
+    ("s", "x", 4, 1), ("s", "x", 4, -1), ("w", "x", 1, 2), ("w", "x", -2, 1), ("c", 1), ("w", "x", -1, 1),
+    ("w", "x", -2, -1), ("c", -1), ("w", "x", 3, 2), ("w", "x", 2, -1), ("w", "x", 3, -1), ("c", 3),
+    ("w", "x", -3, 1), ("w", "x", -3, 2), ("c", -3), ("w", "bz", -2), ("w", "bz", 2), ("c", 2), ("w", "x", -2, 2),
+    ("c", -2), ("w", "x", 4, 1), ("w", "bz", 4), ("w", "x", 4, -1), ("w", "x", 4, 2), ("c", 4),
+)
+
 
 def merge(stats, count):
     means, squares = stats[:, 0], stats[:, 1]
@@ -31,7 +51,7 @@
     pair_send, pair_recv, rs_send, rs_recv, g, stats_z, stats_x,
     load_sem, pair_ssem, pair_rsem, rs_ssem, rs_rsem, gx_ssem, gx_rsem, gz_ssem, gz_rsem,
     sx_ssem, sx_rsem, sz_ssem, sz_rsem,
-    a_rsem, bx_rsem, bz_rsem, ag_ssem,
+    ag_ssem, ag_rsem,
 ):
     row, col = lax.axis_index("row"), lax.axis_index("col")
     y, core = row // 2, row % 2
@@ -156,73 +176,70 @@
 
     last = pl.ds(X_FIRST, wide - X_FIRST)
     first = pl.ds(0, X_FIRST)
-    count = [0]
-
-    def push(ref, rsem, peer):
-        sends.append(send(ref, ref, ag_ssem.at[count[0]], rsem, peer))
-        count[0] += 1
-
-    def push_x(dz):
-        slot = zs(dz) * NX + x
-        for e in STEPS_X:
-            push(g.at[slot, last], a_rsem.at[slot], at(z, xs(e)))
+    middle = X_FIRST + 64
+    halves = {3: pl.ds(X_FIRST, 64), -3: pl.ds(middle, wide - middle)}
+
+    def place(dz, dx):
+        return zs(dz) * NX + xs(dx)
 
     def group(dz):
         return g.at[pl.ds(zs(dz) * NX, NX), first]
 
-    for e in STEPS_X:
-        push(g.at[col, first], bx_rsem.at[x], at(z, xs(e)))
-    for d in STEPS_Z:
-        push(g.at[col, last], a_rsem.at[col], at(zs(d), x))
-
-    push_x(0)
-
-    values = stream.astype(F32)
-    mean = jnp.mean(values, axis=0, keepdims=True)
-    off = values - mean
-    stats_z[z] = jnp.concatenate([mean, jnp.sum(off * off, axis=0, keepdims=True)], axis=0)
-    over_z(stats_z.at[z], sz_ssem, sz_rsem)
-    stream_out[...] = stream
-
-    for e in STEPS_X:
-        arrived(g.at[z * NX + xs(e), first], bx_rsem.at[xs(e)])
-    for d in (4, 3, -3, 2, -2, 1, -1):
-        push(group(0), bz_rsem.at[z], at(zs(d), x))
-
-    def from_z(d):
-        slot = zs(d) * NX + x
-        arrived(g.at[slot, last], a_rsem.at[slot])
-        push_x(d)
-
-    for d in STEPS_Z[:4]:
-        from_z(d)
-    for d in STEPS_Z:
-        arrived(stats_z.at[zs(d)], sz_rsem.at[zs(d)])
-    stats_x[x] = merge(stats_z[...], wide)
-    over_x(stats_x.at[x], sx_ssem, sx_rsem)
-    for d in STEPS_Z[4:]:
-        from_z(d)
-
-    for d in STEPS_Z:
-        arrived(gains.at[pl.ds(zs(d) * NX, NX)], gz_rsem.at[zs(d)])
-    for c in range(NZ):
-        gain_rows[c] = jnp.concatenate([gains[c * NX + k] for k in range(NX)], axis=1)
-
-    for e in STEPS_X:
-        arrived(stats_x.at[xs(e)], sx_rsem.at[xs(e)])
-    both = merge(stats_x[...], NZ * wide)
-    scale = 1.0 / jnp.sqrt(both[1:] * (1.0 / (COLS * wide)) + 1e-6)
-    mean_t = jnp.transpose(jnp.broadcast_to(both[:1], (TOK, TOK)))
-    scale_t = jnp.transpose(jnp.broadcast_to(scale, (TOK, TOK)))
-    c_w.wait()
-
-    for i, d in enumerate((0,) + STEPS_Z):
+    def sent(kind, step):
+        if kind == "z":
+            return g.at[col, last], at(zs(step[0]), x)
+        if kind == "z4":
+            return g.at[place(-step[0], 0), halves[step[0]]], at(zs(step[0] // 3), x)
+        if kind == "bx":
+            return g.at[col, first], at(z, xs(step[0]))
+        if kind == "bz":
+            return group(0), at(zs(step[0]), x)
+        return g.at[place(-step[0], 0), last], at(z, xs(step[1]))
+
+    def received(kind, step):
+        if kind == "z":
+            return g.at[place(-step[0], 0), last]
+        if kind == "z4":
+            return g.at[place(4, 0), halves[step[0]]]
+        if kind == "bx":
+            return g.at[place(0, -step[0]), first]
+        if kind == "bz":
+            return group(-step[0])
+        return g.at[place(-step[0], -step[1]), last]
+
+    copies = [op[1:] for op in ORDER if op[0] == "s"]
+    computes = [op[1] for op in ORDER if op[0] == "c"]
+
+    def share_statistics():
+        values = stream.astype(F32)
+        mean = jnp.mean(values, axis=0, keepdims=True)
+        off = values - mean
+        stats_z[z] = jnp.concatenate([mean, jnp.sum(off * off, axis=0, keepdims=True)], axis=0)
+        over_z(stats_z.at[z], sz_ssem, sz_rsem)
+        stream_out[...] = stream
+
+    def merge_statistics():
+        for d in STEPS_Z:
+            arrived(stats_z.at[zs(d)], sz_rsem.at[zs(d)])
+        stats_x[x] = merge(stats_z[...], wide)
+        over_x(stats_x.at[x], sx_ssem, sx_rsem)
+
+    def before_compute():
+        for d in STEPS_Z:
+            arrived(gains.at[pl.ds(zs(d) * NX, NX)], gz_rsem.at[zs(d)])
+        for c in range(NZ):
+            gain_rows[c] = jnp.concatenate([gains[c * NX + k] for k in range(NX)], axis=1)
         for e in STEPS_X:
-            slot = zs(d) * NX + xs(e)
-            arrived(g.at[slot, last], a_rsem.at[slot])
-        if d:
-            arrived(group(d), bz_rsem.at[zs(d)])
-        zz = zs(d)
+            arrived(stats_x.at[xs(e)], sx_rsem.at[xs(e)])
+        both = merge(stats_x[...], NZ * wide)
+        scale = 1.0 / jnp.sqrt(both[1:] * (1.0 / (COLS * wide)) + 1e-6)
+        mean_t = jnp.transpose(jnp.broadcast_to(both[:1], (TOK, TOK)))
+        scale_t = jnp.transpose(jnp.broadcast_to(scale, (TOK, TOK)))
+        c_w.wait()
+        return mean_t, scale_t
+
+    def project_group(d, mean_t, scale_t):
+        zz = zs(-d)
         block = g[pl.ds(zz * NX, NX)].reshape(NX * wide, TOK)
         tokens = jnp.transpose(block)
         row_gain = gain_rows[zz]
@@ -232,12 +249,32 @@
             piece = (tokens[:, lanes].astype(F32) - mean_t) * scale_t * row_gain[:, lanes]
             pieces.append(piece.astype(BF16))
         out = jnp.dot(jnp.concatenate(pieces, axis=1), w_v[zz], preferred_element_type=F32)
-        if i == 0:
+        if d == computes[0]:
             qk_v[...] = out
-        elif i < NZ - 1:
+        elif d != computes[-1]:
             qk_v[...] += out
         else:
             qk_out[...] = (qk_v[...] + out).astype(BF16)
+
+    moments = None
+    started = 0
+    for op, kind, *step in ORDER:
+        if op == "c":
+            if moments is None:
+                moments = before_compute()
+            project_group(kind, *moments)
+            continue
+        number = copies.index((kind, *step))
+        if op == "s":
+            ref, peer = sent(kind, step)
+            sends.append(send(ref, ref, ag_ssem.at[number], ag_rsem.at[number], peer))
+            started += 1
+            if started == SHARE_AT:
+                share_statistics()
+        else:
+            arrived(received(kind, step), ag_rsem.at[number])
+            if (kind, *step) == MERGE_AT:
+                merge_statistics()
 
     for copy in sends:
         copy.wait_send()
@@ -285,8 +322,7 @@
             dma((NY,)), dma((NY,)), dma((NY - 1,)), dma((NY - 1,)),
             dma((NX - 1,)), dma((NX,)), dma((NZ - 1,)), dma((NZ,)),
             dma((NX - 1,)), dma((NX,)), dma((NZ - 1,)), dma((NZ,)),
-            dma((COLS,)), dma((NX,)), dma((NZ,)),
-            dma((48,)),
+            dma((48,)), dma((48,)),
         ],
         compiler_params=pltpu.CompilerParams(
             collective_id=0, has_side_effects=True, vmem_limit_bytes=56 * 1024 * 1024

time: 37.1 us -> 36.7 us (0.989)
  Pallas kernels: 36.3 us -> 35.7 us
    pallas_call x1, Pallas kernels: 35.6 us -> 35 us  [per_device(): pl.pallas_call(kernel, out_shape=(pltpu.VMEM((width, TOK), BF16), pltpu.V...]
where the time goes in v5:
time: 36.7 us; the launch traced here: 36.4 us
  Pallas kernels  35.7 us (97%)
  between operations  0.64 us (2%)
    pallas_call x1, Pallas kernels, per_device(): pl.pallas_call(kernel, out_shape=(pltpu.VMEM((width, TOK), BF16), pltpu.V...  35 us

profile of v5, /device:TPU:2, one launch (start us, length us, event | category | flops | bytes accessed | tf_op | source)
XLA Modules:
  0.0 36.4 jit_solution(12309992063845536282)
XLA Ops:
  0.6 35.0 %shard_map.68 = (bf16[192,128]{1,0:T(8,128)(2,1)S(1)}, bf16[128,384]{1,0:T(8,128)(2,1)S(1)}) custom-call(bf16[1024,3072]{1,0:T(8,128)(2,1)} %hidden.1, bf16[192,3072]{1,0:T(8,128)(2,1)} %bitcast.5, bf16[192,128]{1,0:T(8,128)(2,1)} %bitcast.6, bf16[192]{0:T(256)(128)(2,1)} %gain.1, bf16[8,768,384]{2,1,0:T(8,128)(2,1)} %bitcast.4), custom_call_target="tpu_custom_call" | custom-call | tf_op jit(solution)/shard_map/pallas_call | solution.py:300
  35.7 0.7 %shard_map.69 = (bf16[192,128]{1,0:T(8,128)(2,1)}, bf16[128,384]{1,0:T(8,128)(2,1)}) custom-call(bf16[192,128]{1,0:T(8,128)(2,1)S(1)} %get-tuple-element.6.stream, bf16[128,384]{1,0:T(8,128)(2,1)S(1)} %get-tuple-element.7.queries_keys), custom_call_target="tpu_custom_call" | custom-call | tf_op jit(solution)/shard_map/pallas_call | solution.py:334

commit v6 on v5

v6 whole, which is shorter than its diff:
```python
import functools

import jax
import jax.numpy as jnp
from jax import lax
from jax.experimental import pallas as pl
from jax.experimental.pallas import tpu as pltpu
from jax.sharding import PartitionSpec as P

MESH = pl.DeviceIdType.MESH
F32, BF16 = jnp.float32, jnp.bfloat16
NX, NZ, NY = 4, 8, 4
ROWS, COLS = 2 * NY, NZ * NX
TOK = 128
CUTS = 3
X_FIRST = 48
STEPS_Z = (1, -1, 2, -2, 3, -3, 4)
STEPS_X = (1, -1, 2)

SHARE_AT = 12
MERGE_AT = ("z", -2)
ORDER = (
    ("s", "z", 1), ("s", "z", -1), ("s", "bx", 2), ("s", "x", 0, -1), ("s", "bx", -1), ("s", "z", 2), ("s", "z", 3),
    ("s", "bx", 1), ("s", "z", -3), ("s", "z", -2), ("s", "x", 0, 2), ("s", "x", 0, 1), ("w", "z", 1),
    ("s", "x", 1, 2), ("w", "z", -1), ("s", "x", 1, -1), ("s", "x", 1, 1), ("s", "x", -1, 2), ("s", "x", -1, -1),
    ("w", "bx"), ("s", "bz", -3), ("s", "bz", 3), ("s", "bz", -1), ("s", "x", -1, 1), ("s", "bz", 1), ("w", "z", 2),
    ("s", "x", 2, 2), ("s", "x", 2, 1), ("s", "x", 2, -1), ("w", "z", 3), ("s", "x", 3, 1), ("w", "z", -3),
    ("s", "z4", 3), ("s", "x", -3, -1), ("w", "z", -2), ("s", "z4", -3), ("s", "bz", 2), ("s", "bz", -2),
    ("s", "x", 3, 2), ("s", "x", -2, 1), ("s", "x", -2, -1), ("s", "bz", 4), ("s", "x", -3, 2), ("s", "x", -3, 1),
    ("s", "x", 3, -1), ("s", "x", -2, 2), ("w", "z4"), ("s", "x", 4, 2), ("s", "x", 4, 1),
    ("s", "x", 4, -1), ("c", 0), ("c", 1), ("c", -1), ("c", 3), ("c", -3), ("c", 2), ("c", -2), ("c", 4),
)


def merge(stats, count):
    means, squares = stats[:, 0], stats[:, 1]
    mean = jnp.mean(means, axis=0, keepdims=True)
    off = means - mean
    square = jnp.sum(squares, axis=0, keepdims=True) + count * jnp.sum(off * off, axis=0, keepdims=True)
    return jnp.concatenate([mean, square], axis=0)


def kernel(
    hidden, down, residual, gain, weight, stream_out, qk_out,
    hid_v, down_v, acc, res_v, gain_in, gains, gain_rows, w_v, qk_v,
    pair_send, pair_recv, rs_send, rs_recv, g, stats_z, stats_x,
    load_sem, pair_ssem, pair_rsem, rs_ssem, rs_rsem, gx_ssem, gx_rsem, gz_ssem, gz_rsem,
    sx_ssem, sx_rsem, sz_ssem, sz_rsem,
    ag_ssem, z_rsem, bx_rsem, bz_rsem, x_rsem,
):
    row, col = lax.axis_index("row"), lax.axis_index("col")
    y, core = row // 2, row % 2
    z, x = col // NX, col % NX
    wide = down.shape[0]

    def at(zz, xx):
        return (row, zz * NX + xx)

    def zs(d):
        return lax.rem(z + d + NZ, NZ)

    def xs(d):
        return lax.rem(x + d + NX, NX)

    def load(src, dst, sem):
        copy = pltpu.make_async_copy(src, dst, load_sem.at[sem])
        copy.start()
        return copy

    step = down.shape[1] // CUTS
    c_gain = load(gain, gain_in, 0)
    c_down, c_half = [], ([], [])
    for k in range(CUTS):
        span = slice(k * step, (k + 1) * step)
        c_down.append(load(down.at[:, span], down_v.at[:, span], 4 + k))
        c_half[0].append(load(hidden.at[:, 1 - core, :, span], hid_v.at[0, :, :, span], 4 + CUTS + k))
    for k in range(CUTS):
        span = slice(k * step, (k + 1) * step)
        c_half[1].append(load(hidden.at[:, core, :, span], hid_v.at[1, :, :, span], 4 + 2 * CUTS + k))

    barrier = pltpu.get_barrier_semaphore()
    sibling = (y * 2 + 1 - core, col)
    peers = [sibling] + [(lax.rem(y + d, NY) * 2 + core, col) for d in range(1, NY)]
    peers += [at(z, xs(d)) for d in STEPS_X]
    peers += [at(zs(d), x) for d in STEPS_Z]
    for peer in peers:
        pl.semaphore_signal(barrier, inc=1, device_id=peer, device_id_type=MESH)

    def send(src, dst, ssem, rsem, peer):
        copy = pltpu.make_async_remote_copy(
            src_ref=src, dst_ref=dst, send_sem=ssem, recv_sem=rsem,
            device_id=peer, device_id_type=MESH,
        )
        copy.start()

    def arrived(ref, rsem):
        pltpu.make_async_copy(ref, ref, rsem).wait()

    def over_x(ref, ssem, rsem):
        for d in STEPS_X:
            send(ref, ref, ssem, rsem, at(z, xs(d)))

    def over_z(ref, ssem, rsem):
        for d in STEPS_Z:
            send(ref, ref, ssem, rsem, at(zs(d), x))

    def project(half):
        for k in range(CUTS):
            span = slice(k * step, (k + 1) * step)
            if half == 0:
                c_down[k].wait()
            c_half[half][k].wait()
            tokens = hid_v[half, :, :, span].reshape(NY * TOK, step)
            part = lax.dot_general(
                down_v[:, span], tokens, (((1,), (1,)), ((), ())), preferred_element_type=F32
            )
            if k == 0:
                acc[...] = part
            else:
                acc[...] += part

    project(0)
    for k in range(NY):
        pair_send[k] = acc[:, k * TOK:(k + 1) * TOK].astype(BF16)
    c_gain.wait()
    gains[col] = gain_in[...].astype(F32).reshape(1, wide)
    pl.semaphore_wait(barrier, len(peers))
    send(pair_send, pair_recv, pair_ssem, pair_rsem, sibling)
    over_x(gains.at[col], gx_ssem, gx_rsem)
    c_res = load(residual, res_v, 1)
    project(1)
    arrived(pair_recv, pair_rsem)
    for k in range(NY):
        acc[:, k * TOK:(k + 1) * TOK] += pair_recv[k].astype(F32)
    for d in (2, 1, 3):
        yy = lax.rem(y + d, NY)
        piece = acc[:, pl.ds(pl.multiple_of(yy * TOK, TOK), TOK)]
        rs_send[d - 1] = piece.astype(BF16)
        peer = (yy * 2 + core, col)
        send(rs_send.at[d - 1], rs_recv.at[NY - 1 - d], rs_ssem, rs_rsem, peer)
    own = acc[:, pl.ds(pl.multiple_of(y * TOK, TOK), TOK)]

    c_w = load(weight, w_v, 2)

    arrived(gains.at[pl.ds(0, NX - 1)], gx_rsem)
    over_z(gains.at[pl.ds(z * NX, NX)], gz_ssem, gz_rsem)
    c_res.wait()
    total = res_v[...].astype(F32) + own
    arrived(rs_recv, rs_rsem)
    for d in range(NY - 1):
        total = total + rs_recv[d].astype(F32)
    stream = total.astype(BF16)
    g[col] = stream

    last = pl.ds(X_FIRST, wide - X_FIRST)
    first = pl.ds(0, X_FIRST)
    middle = X_FIRST + 64
    halves = {3: pl.ds(X_FIRST, 64), -3: pl.ds(middle, wide - middle)}

    def place(dz, dx):
        return zs(dz) * NX + xs(dx)

    def group(dz):
        return g.at[pl.ds(zs(dz) * NX, NX), first]

    def sent(kind, step):
        if kind == "z":
            return g.at[col, last], at(zs(step[0]), x)
        if kind == "z4":
            return g.at[place(-step[0], 0), halves[step[0]]], at(zs(step[0] // 3), x)
        if kind == "bx":
            return g.at[col, first], at(z, xs(step[0]))
        if kind == "bz":
            return group(0), at(zs(step[0]), x)
        return g.at[place(-step[0], 0), last], at(z, xs(step[1]))

    z_steps = STEPS_Z[:-1]
    groups = (0,) + STEPS_Z

    def semaphore(kind, step):
        if kind == "z":
            return z_rsem.at[z_steps.index(step[0])]
        if kind == "z4":
            return z_rsem.at[len(z_steps)]
        if kind == "bx":
            return bx_rsem
        if kind == "bz":
            return bz_rsem.at[STEPS_Z.index(step[0])]
        return x_rsem.at[groups.index(step[0])]

    def take(kind, step):
        if kind == "z":
            arrived(g.at[place(-step[0], 0), last], semaphore(kind, step))
        elif kind == "z4":
            arrived(g.at[place(4, 0), last], semaphore(kind, step))
        elif kind == "bx":
            arrived(g.at[pl.ds(z * NX, NX - 1), first], semaphore(kind, step))
        elif kind == "bz":
            arrived(group(-step[0]), semaphore(kind, step))
        else:
            arrived(g.at[pl.ds(zs(-step[0]) * NX, NX - 1), last], semaphore(kind, step))

    computes = [op[1] for op in ORDER if op[0] == "c"]

    def share_statistics():
        values = stream.astype(F32)
        mean = jnp.mean(values, axis=0, keepdims=True)
        off = values - mean
        stats_z[z] = jnp.concatenate([mean, jnp.sum(off * off, axis=0, keepdims=True)], axis=0)
        over_z(stats_z.at[z], sz_ssem, sz_rsem)
        stream_out[...] = stream

    def merge_statistics():
        arrived(stats_z.at[pl.ds(0, NZ - 1)], sz_rsem)
        stats_x[x] = merge(stats_z[...], wide)
        over_x(stats_x.at[x], sx_ssem, sx_rsem)

    def before_compute():
        arrived(gains.at[pl.ds(0, COLS - NX)], gz_rsem)
        for c in range(NZ):
            gain_rows[c] = jnp.concatenate([gains[c * NX + k] for k in range(NX)], axis=1)
        arrived(stats_x.at[pl.ds(0, NX - 1)], sx_rsem)
        both = merge(stats_x[...], NZ * wide)
        scale = 1.0 / jnp.sqrt(both[1:] * (1.0 / (COLS * wide)) + 1e-6)
        mean_t = jnp.transpose(jnp.broadcast_to(both[:1], (TOK, TOK)))
        scale_t = jnp.transpose(jnp.broadcast_to(scale, (TOK, TOK)))
        c_w.wait()
        return mean_t, scale_t

    def project_group(d, mean_t, scale_t):
        zz = zs(-d)
        block = g[pl.ds(zz * NX, NX)].reshape(NX * wide, TOK)
        tokens = jnp.transpose(block)
        row_gain = gain_rows[zz]
        pieces = []
        for k in range(NX * wide // TOK):
            lanes = slice(k * TOK, (k + 1) * TOK)
            piece = (tokens[:, lanes].astype(F32) - mean_t) * scale_t * row_gain[:, lanes]
            pieces.append(piece.astype(BF16))
        out = jnp.dot(jnp.concatenate(pieces, axis=1), w_v[zz], preferred_element_type=F32)
        if d == computes[0]:
            qk_v[...] = out
        elif d != computes[-1]:
            qk_v[...] += out
        else:
            qk_out[...] = (qk_v[...] + out).astype(BF16)

    moments = None
    started = 0
    for op, kind, *step in ORDER:
        if op == "c":
            if moments is None:
                moments = before_compute()
            take("x", (kind,))
            if kind:
                take("bz", (kind,))
            project_group(kind, *moments)
        elif op == "s":
            ref, peer = sent(kind, step)
            send(ref, ref, ag_ssem, semaphore(kind, step), peer)
            started += 1
            if started == SHARE_AT:
                share_statistics()
        else:
            take(kind, step)
            if (kind, *step) == MERGE_AT:
                merge_statistics()

    arrived(pair_send, pair_ssem)
    arrived(rs_send, rs_ssem)
    arrived(gains.at[pl.ds(0, NX - 1)], gx_ssem)
    arrived(gains.at[pl.ds(0, COLS - NX)], gz_ssem)
    arrived(stats_z.at[pl.ds(0, NZ - 1)], sz_ssem)
    arrived(stats_x.at[pl.ds(0, NX - 1)], sx_ssem)
    arrived(g.at[pl.ds(0, COLS - 1)], ag_ssem)


def deliver(stream, queries_keys, stream_out, qk_out, sem):
    copies = [
        pltpu.make_async_copy(stream, stream_out, sem.at[0]),
        pltpu.make_async_copy(queries_keys, qk_out, sem.at[1]),
    ]
    for copy in copies:
        copy.start()
    for copy in copies:
        copy.wait()


def per_device(hidden, down_weight, residual, gain, qk_weight):
    depth, width = down_weight.shape
    full, heads = qk_weight.shape
    vmem_spec = pl.BlockSpec(memory_space=pltpu.VMEM)
    any_spec = pl.BlockSpec(memory_space=pl.ANY)
    dma = pltpu.SemaphoreType.DMA
    stream, queries_keys = pl.pallas_call(
        kernel,
        out_shape=(pltpu.VMEM((width, TOK), BF16), pltpu.VMEM((TOK, heads), BF16)),
        in_specs=[any_spec] * 5,
        out_specs=(vmem_spec, vmem_spec),
        scratch_shapes=[
            pltpu.VMEM((2, NY, TOK, depth), BF16),
            pltpu.VMEM((width, depth), BF16),
            pltpu.VMEM((width, NY * TOK), F32),
            pltpu.VMEM((width, TOK), BF16),
            pltpu.VMEM((width,), BF16),
            pltpu.VMEM((COLS, 1, width), F32),
            pltpu.VMEM((NZ, 1, NX * width), F32),
            pltpu.VMEM((NZ, NX * width, heads), BF16),
            pltpu.VMEM((TOK, heads), F32),
            pltpu.VMEM((NY, width, TOK), BF16),
            pltpu.VMEM((NY, width, TOK), BF16),
            pltpu.VMEM((NY - 1, width, TOK), BF16),
            pltpu.VMEM((NY - 1, width, TOK), BF16),
            pltpu.VMEM((COLS, width, TOK), BF16),
            pltpu.VMEM((NZ, 2, TOK), F32),
            pltpu.VMEM((NX, 2, TOK), F32),
            dma((4 + 3 * CUTS,)),
            *[dma(())] * 12,
            dma(()), dma((NZ - 1,)), dma(()), dma((NZ - 1,)), dma((NZ,)),
        ],
        compiler_params=pltpu.CompilerParams(
            collective_id=0, has_side_effects=True, vmem_limit_bytes=56 * 1024 * 1024
        ),
    )(
        hidden.reshape(NY, 2, TOK, depth), down_weight.T, residual.T, gain,
        qk_weight.reshape(NZ, NX * width, heads),
    )
    stream, queries_keys = pl.pallas_call(
        deliver,
        out_shape=(
            jax.ShapeDtypeStruct((width, TOK), BF16),
            jax.ShapeDtypeStruct((TOK, heads), BF16),
        ),
        in_specs=[vmem_spec] * 2,
        out_specs=(any_spec, any_spec),
        scratch_shapes=[dma((2,))],
    )(
        pltpu.with_memory_space_constraint(stream, pltpu.VMEM),
        pltpu.with_memory_space_constraint(queries_keys, pltpu.VMEM),
    )
    return stream.T, queries_keys


def solution(mesh):
    placed = (P(None, "row"), P("row", "col"), P("row", "col"), P("col"), P(None, "col"))
    return jax.shard_map(
        per_device,
        mesh=mesh,
        in_specs=placed,
        out_specs=(P("row", "col"), P("row", "col")),
        check_vma=False,
    )
```

time: 36.7 us -> 34.5 us (0.940)
  Pallas kernels: 35.7 us -> 33.7 us
    pallas_call x1, Pallas kernels: 35 us -> 33.1 us  [per_device(): pl.pallas_call(kernel, out_shape=(pltpu.VMEM((width, TOK), BF16), pltpu.V...]
where the time goes in v6:
time: 34.5 us; the launch traced here: 34.4 us
  Pallas kernels  33.7 us (98%)
  between operations  0.64 us (2%)
    pallas_call x1, Pallas kernels, per_device(): pl.pallas_call(kernel, out_shape=(pltpu.VMEM((width, TOK), BF16), pltpu.V...  33.1 us

profile of v6, /device:TPU:2, one launch (start us, length us, event | category | flops | bytes accessed | tf_op | source)
XLA Modules:
  0.0 34.4 jit_solution(16476940058551595249)
XLA Ops:
  0.6 33.1 %shard_map.68 = (bf16[192,128]{1,0:T(8,128)(2,1)S(1)}, bf16[128,384]{1,0:T(8,128)(2,1)S(1)}) custom-call(bf16[4,2,128,3072]{3,2,1,0:T(8,128)(2,1)} %bitcast.5, bf16[192,3072]{1,0:T(8,128)(2,1)} %bitcast.7, bf16[192,128]{1,0:T(8,128)(2,1)} %bitcast.8, bf16[192]{0:T(256)(128)(2,1)} %gain.1, bf16[8,768,384]{2,1,0:T(8,128)(2,1)} %bitcast.6), custom_call_target="tpu_custom_call" | custom-call | tf_op jit(solution)/shard_map/pallas_call | solution.py:295
  33.7 0.7 %shard_map.69 = (bf16[192,128]{1,0:T(8,128)(2,1)}, bf16[128,384]{1,0:T(8,128)(2,1)}) custom-call(bf16[192,128]{1,0:T(8,128)(2,1)S(1)} %get-tuple-element.6.stream, bf16[128,384]{1,0:T(8,128)(2,1)S(1)} %get-tuple-element.7.queries_keys), custom_call_target="tpu_custom_call" | custom-call | tf_op jit(solution)/shard_map/pallas_call | solution.py:328

commit v7 on v6

--- a/solution.py
+++ b/solution.py
@@ -12,7 +12,7 @@
 NX, NZ, NY = 4, 8, 4
 ROWS, COLS = 2 * NY, NZ * NX
 TOK = 128
-CUTS = 3
+CUTS = 4
 X_FIRST = 48
 STEPS_Z = (1, -1, 2, -2, 3, -3, 4)
 STEPS_X = (1, -1, 2)
@@ -209,6 +209,9 @@
         stats_z[z] = jnp.concatenate([mean, jnp.sum(off * off, axis=0, keepdims=True)], axis=0)
         over_z(stats_z.at[z], sz_ssem, sz_rsem)
         stream_out[...] = stream
+        arrived(gains.at[pl.ds(0, COLS - NX)], gz_rsem)
+        for c in range(NZ):
+            gain_rows[c] = jnp.concatenate([gains[c * NX + k] for k in range(NX)], axis=1)
 
     def merge_statistics():
         arrived(stats_z.at[pl.ds(0, NZ - 1)], sz_rsem)
@@ -216,9 +219,6 @@
         over_x(stats_x.at[x], sx_ssem, sx_rsem)
 
     def before_compute():
-        arrived(gains.at[pl.ds(0, COLS - NX)], gz_rsem)
-        for c in range(NZ):
-            gain_rows[c] = jnp.concatenate([gains[c * NX + k] for k in range(NX)], axis=1)
         arrived(stats_x.at[pl.ds(0, NX - 1)], sx_rsem)
         both = merge(stats_x[...], NZ * wide)
         scale = 1.0 / jnp.sqrt(both[1:] * (1.0 / (COLS * wide)) + 1e-6)

time: 34.5 us -> 34.4 us (level)
  no operation moved by 1% of the time
where the time goes in v7:
time: 34.4 us; the launch traced here: 34.2 us
  Pallas kernels  33.6 us (98%)
  between operations  0.64 us (2%)
    pallas_call x1, Pallas kernels, per_device(): pl.pallas_call(kernel, out_shape=(pltpu.VMEM((width, TOK), BF16), pltpu.V...  32.9 us

profile of v7, /device:TPU:2, one launch (start us, length us, event | category | flops | bytes accessed | tf_op | source)
XLA Modules:
  0.0 34.2 jit_solution(4401013167511829414)
XLA Ops:
  0.6 32.9 %shard_map.68 = (bf16[192,128]{1,0:T(8,128)(2,1)S(1)}, bf16[128,384]{1,0:T(8,128)(2,1)S(1)}) custom-call(bf16[4,2,128,3072]{3,2,1,0:T(8,128)(2,1)} %bitcast.5, bf16[192,3072]{1,0:T(8,128)(2,1)} %bitcast.7, bf16[192,128]{1,0:T(8,128)(2,1)} %bitcast.8, bf16[192]{0:T(256)(128)(2,1)} %gain.1, bf16[8,768,384]{2,1,0:T(8,128)(2,1)} %bitcast.6), custom_call_target="tpu_custom_call" | custom-call | tf_op jit(solution)/shard_map/pallas_call | solution.py:295
  33.6 0.7 %shard_map.69 = (bf16[192,128]{1,0:T(8,128)(2,1)}, bf16[128,384]{1,0:T(8,128)(2,1)}) custom-call(bf16[192,128]{1,0:T(8,128)(2,1)S(1)} %get-tuple-element.6.stream, bf16[128,384]{1,0:T(8,128)(2,1)S(1)} %get-tuple-element.7.queries_keys), custom_call_target="tpu_custom_call" | custom-call | tf_op jit(solution)/shard_map/pallas_call | solution.py:328

commit v8 on v7

--- a/solution.py
+++ b/solution.py
@@ -67,6 +67,14 @@
         copy.start()
         return copy
 
+    barrier = pltpu.get_barrier_semaphore()
+    sibling = (y * 2 + 1 - core, col)
+    peers = [sibling] + [(lax.rem(y + d, NY) * 2 + core, col) for d in range(1, NY)]
+    peers += [at(z, xs(d)) for d in STEPS_X]
+    peers += [at(zs(d), x) for d in STEPS_Z]
+    for peer in peers:
+        pl.semaphore_signal(barrier, inc=1, device_id=peer, device_id_type=MESH)
+
     step = down.shape[1] // CUTS
     c_gain = load(gain, gain_in, 0)
     c_down, c_half = [], ([], [])
@@ -77,14 +85,6 @@
     for k in range(CUTS):
         span = slice(k * step, (k + 1) * step)
         c_half[1].append(load(hidden.at[:, core, :, span], hid_v.at[1, :, :, span], 4 + 2 * CUTS + k))
-
-    barrier = pltpu.get_barrier_semaphore()
-    sibling = (y * 2 + 1 - core, col)
-    peers = [sibling] + [(lax.rem(y + d, NY) * 2 + core, col) for d in range(1, NY)]
-    peers += [at(z, xs(d)) for d in STEPS_X]
-    peers += [at(zs(d), x) for d in STEPS_Z]
-    for peer in peers:
-        pl.semaphore_signal(barrier, inc=1, device_id=peer, device_id_type=MESH)
 
     def send(src, dst, ssem, rsem, peer):
         copy = pltpu.make_async_remote_copy(
@@ -130,15 +130,17 @@
     c_res = load(residual, res_v, 1)
     project(1)
     arrived(pair_recv, pair_rsem)
-    for k in range(NY):
-        acc[:, k * TOK:(k + 1) * TOK] += pair_recv[k].astype(F32)
+
+    def summed(place):
+        return acc[:, pl.ds(pl.multiple_of(place * TOK, TOK), TOK)] + pair_recv[place].astype(F32)
+
     for d in (2, 1, 3):
         yy = lax.rem(y + d, NY)
-        piece = acc[:, pl.ds(pl.multiple_of(yy * TOK, TOK), TOK)]
+        piece = summed(yy)
         rs_send[d - 1] = piece.astype(BF16)
         peer = (yy * 2 + core, col)
         send(rs_send.at[d - 1], rs_recv.at[NY - 1 - d], rs_ssem, rs_rsem, peer)
-    own = acc[:, pl.ds(pl.multiple_of(y * TOK, TOK), TOK)]
+    own = summed(y)
 
     c_w = load(weight, w_v, 2)
 

time: 34.4 us -> 34.5 us (level)
  no operation moved by 1% of the time
where the time goes in v8:
time: 34.5 us; the launch traced here: 34.4 us
  Pallas kernels  33.8 us (98%)
  between operations  0.64 us (2%)
    pallas_call x1, Pallas kernels, per_device(): pl.pallas_call(kernel, out_shape=(pltpu.VMEM((width, TOK), BF16), pltpu.V...  33.1 us

profile of v8, /device:TPU:2, one launch (start us, length us, event | category | flops | bytes accessed | tf_op | source)
XLA Modules:
  0.0 34.4 jit_solution(8099294807439129364)
XLA Ops:
  0.6 33.1 %shard_map.68 = (bf16[192,128]{1,0:T(8,128)(2,1)S(1)}, bf16[128,384]{1,0:T(8,128)(2,1)S(1)}) custom-call(bf16[4,2,128,3072]{3,2,1,0:T(8,128)(2,1)} %bitcast.5, bf16[192,3072]{1,0:T(8,128)(2,1)} %bitcast.7, bf16[192,128]{1,0:T(8,128)(2,1)} %bitcast.8, bf16[192]{0:T(256)(128)(2,1)} %gain.1, bf16[8,768,384]{2,1,0:T(8,128)(2,1)} %bitcast.6), custom_call_target="tpu_custom_call" | custom-call | tf_op jit(solution)/shard_map/pallas_call | solution.py:297
  33.8 0.7 %shard_map.69 = (bf16[192,128]{1,0:T(8,128)(2,1)}, bf16[128,384]{1,0:T(8,128)(2,1)}) custom-call(bf16[192,128]{1,0:T(8,128)(2,1)S(1)} %get-tuple-element.6.stream, bf16[128,384]{1,0:T(8,128)(2,1)S(1)} %get-tuple-element.7.queries_keys), custom_call_target="tpu_custom_call" | custom-call | tf_op jit(solution)/shard_map/pallas_call | solution.py:330

commit v9 on v7

--- a/solution.py
+++ b/solution.py
@@ -130,17 +130,17 @@
     c_res = load(residual, res_v, 1)
     project(1)
     arrived(pair_recv, pair_rsem)
-    for k in range(NY):
-        acc[:, k * TOK:(k + 1) * TOK] += pair_recv[k].astype(F32)
+
+    def summed(place):
+        return acc[:, pl.ds(pl.multiple_of(place * TOK, TOK), TOK)] + pair_recv[place].astype(F32)
+
     for d in (2, 1, 3):
         yy = lax.rem(y + d, NY)
-        piece = acc[:, pl.ds(pl.multiple_of(yy * TOK, TOK), TOK)]
+        piece = summed(yy)
         rs_send[d - 1] = piece.astype(BF16)
         peer = (yy * 2 + core, col)
         send(rs_send.at[d - 1], rs_recv.at[NY - 1 - d], rs_ssem, rs_rsem, peer)
-    own = acc[:, pl.ds(pl.multiple_of(y * TOK, TOK), TOK)]
-
-    c_w = load(weight, w_v, 2)
+    own = summed(y)
 
     arrived(gains.at[pl.ds(0, NX - 1)], gx_rsem)
     over_z(gains.at[pl.ds(z * NX, NX)], gz_ssem, gz_rsem)
@@ -246,6 +246,7 @@
             qk_out[...] = (qk_v[...] + out).astype(BF16)
 
     moments = None
+    c_w = load(weight, w_v, 2)
     started = 0
     for op, kind, *step in ORDER:
         if op == "c":

time: 34.4 us -> 34.4 us (level)
  no operation moved by 1% of the time
where the time goes in v9:
time: 34.4 us; the launch traced here: 34.2 us
  Pallas kernels  33.6 us (98%)
  between operations  0.64 us (2%)
    pallas_call x1, Pallas kernels, per_device(): pl.pallas_call(kernel, out_shape=(pltpu.VMEM((width, TOK), BF16), pltpu.V...  32.9 us

profile of v9, /device:TPU:2, one launch (start us, length us, event | category | flops | bytes accessed | tf_op | source)
XLA Modules:
  0.0 34.2 jit_solution(6656736506047889540)
XLA Ops:
  0.6 32.9 %shard_map.68 = (bf16[192,128]{1,0:T(8,128)(2,1)S(1)}, bf16[128,384]{1,0:T(8,128)(2,1)S(1)}) custom-call(bf16[4,2,128,3072]{3,2,1,0:T(8,128)(2,1)} %bitcast.5, bf16[192,3072]{1,0:T(8,128)(2,1)} %bitcast.7, bf16[192,128]{1,0:T(8,128)(2,1)} %bitcast.8, bf16[192]{0:T(256)(128)(2,1)} %gain.1, bf16[8,768,384]{2,1,0:T(8,128)(2,1)} %bitcast.6), custom_call_target="tpu_custom_call" | custom-call | tf_op jit(solution)/shard_map/pallas_call | solution.py:296
  33.5 0.7 %shard_map.69 = (bf16[192,128]{1,0:T(8,128)(2,1)}, bf16[128,384]{1,0:T(8,128)(2,1)}) custom-call(bf16[192,128]{1,0:T(8,128)(2,1)S(1)} %get-tuple-element.6.stream, bf16[128,384]{1,0:T(8,128)(2,1)S(1)} %get-tuple-element.7.queries_keys), custom_call_target="tpu_custom_call" | custom-call | tf_op jit(solution)/shard_map/pallas_call | solution.py:329

commit v10 on v9

--- a/solution.py
+++ b/solution.py
@@ -141,6 +141,8 @@
         peer = (yy * 2 + core, col)
         send(rs_send.at[d - 1], rs_recv.at[NY - 1 - d], rs_ssem, rs_rsem, peer)
     own = summed(y)
+
+    c_w = load(weight, w_v, 2)
 
     arrived(gains.at[pl.ds(0, NX - 1)], gx_rsem)
     over_z(gains.at[pl.ds(z * NX, NX)], gz_ssem, gz_rsem)
@@ -246,7 +248,6 @@
             qk_out[...] = (qk_v[...] + out).astype(BF16)
 
     moments = None
-    c_w = load(weight, w_v, 2)
     started = 0
     for op, kind, *step in ORDER:
         if op == "c":

time: 34.4 us -> 34.4 us (level)
  no operation moved by 1% of the time
where the time goes in v10:
time: 34.4 us; the launch traced here: 34.2 us
  Pallas kernels  33.6 us (98%)
  between operations  0.64 us (2%)
    pallas_call x1, Pallas kernels, per_device(): pl.pallas_call(kernel, out_shape=(pltpu.VMEM((width, TOK), BF16), pltpu.V...  32.9 us

profile of v10, /device:TPU:2, one launch (start us, length us, event | category | flops | bytes accessed | tf_op | source)
XLA Modules:
  0.0 34.2 jit_solution(14504537784059331220)
XLA Ops:
  0.6 32.9 %shard_map.68 = (bf16[192,128]{1,0:T(8,128)(2,1)S(1)}, bf16[128,384]{1,0:T(8,128)(2,1)S(1)}) custom-call(bf16[4,2,128,3072]{3,2,1,0:T(8,128)(2,1)} %bitcast.5, bf16[192,3072]{1,0:T(8,128)(2,1)} %bitcast.7, bf16[192,128]{1,0:T(8,128)(2,1)} %bitcast.8, bf16[192]{0:T(256)(128)(2,1)} %gain.1, bf16[8,768,384]{2,1,0:T(8,128)(2,1)} %bitcast.6), custom_call_target="tpu_custom_call" | custom-call | tf_op jit(solution)/shard_map/pallas_call | solution.py:297
  33.5 0.7 %shard_map.69 = (bf16[192,128]{1,0:T(8,128)(2,1)}, bf16[128,384]{1,0:T(8,128)(2,1)}) custom-call(bf16[192,128]{1,0:T(8,128)(2,1)S(1)} %get-tuple-element.6.stream, bf16[128,384]{1,0:T(8,128)(2,1)S(1)} %get-tuple-element.7.queries_keys), custom_call_target="tpu_custom_call" | custom-call | tf_op jit(solution)/shard_map/pallas_call | solution.py:330
